TPU v7x, 256 devices: a whole 4x4x8 slice. The times are simulated.
256 devices in a mesh: lat: 16 (over y_lo, x, core), lon: 16 (over y_hi, z).
Axes of the slice: x: 4, y: 4 (y_hi: 2, y_lo: 2; y = y_hi * 2 + y_lo), z: 8, core: 2. Of those that a mesh axis runs over, the one named last changes fastest.
Arguments:
- fields: bfloat16 [32, 128, 4096], P(None, 'lat', 'lon'), may hold values from -6 to 6
- cotangent: bfloat16 [32, 128, 4096], P(None, 'lat', 'lon'), may hold values from -0.008239746 to 0.008239746
- kernel_in: bfloat16 [9, 128, 32], replicated, may hold values from -0.375 to 0.375
- kernel_mid: bfloat16 [9, 128, 128], replicated, may hold values from -0.1875 to 0.1875
- kernel_out: bfloat16 [9, 32, 128], replicated, may hold values from -0.1875 to 0.1875
- patch_anchors: int32 [16, 16, 4, 2], P('lat', 'lon'), may hold values from 0 to 8
- blend_weights: int32 [4, 128, 4096], P(None, 'lat', 'lon'), may hold values from 1 to 8
- tile_counts: int32 [16, 16], P('lat', 'lon'), may hold values from 0 to 4, as said below
Outputs:
- blended: float32 [32, 128, 4096], P(None, 'lat', 'lon')
- grad_in: float32 [9, 128, 32], replicated
- grad_mid: float32 [9, 128, 128], replicated
- grad_out: float32 [9, 32, 128], replicated
Inputs may be any that keep to these rules, and one draw needn't show every extreme that they name: `tile_counts`: the counts of the tiles in lat rows i and i + 8 at the same lon sum to exactly 4; tile (1, 0) holds 4 patches and tile (9, 0) none.
All inputs are finite; a program needn't handle non-finite values.
Results may differ from a plain program's by a relative error of at most 0.005.
Values may be sent and summed in bfloat16 or wider, within the bound.
A program may use at most 64 MiB of HBM per device.

v0:
```python
import jax
import jax.numpy as jnp
from jax import lax
from jax.sharding import PartitionSpec as P

MARGIN = 4
SLOTS = 4


KERNEL_TAPS = ((0, 0), (0, 1), (0, 2), (1, 0), (1, 1), (1, 2), (2, 0), (2, 1), (2, 2))


def extended_2(block, sides, width):
    for axis, dim in sides:
        count = lax.axis_size(axis)
        forward = [(i, i + 1) for i in range(count - 1)]
        forward.append((count - 1, 0))
        backward = [(target, source) for source, target in forward]
        low = lax.ppermute(
            lax.slice_in_dim(block, block.shape[dim] - width, None, axis=dim), axis, forward
        )
        high = lax.ppermute(lax.slice_in_dim(block, 0, width, axis=dim), axis, backward)
        block = jnp.concatenate([low, block, high], axis=dim)
    return block


def shifted(value, axis, steps):
    count = lax.axis_size(axis)
    pairs = [(source, (source + steps) % count) for source in range(count)]
    return lax.ppermute(value, axis, pairs)


def forward_conv(values, kernel):
    height, breadth = (values.shape[1], values.shape[2])
    padded = jnp.pad(values, ((0, 0), (1, 1), (1, 1)))
    summed = jnp.zeros((kernel.shape[1], height, breadth), jnp.float32)
    for tap_index, (tap_row, tap_col) in enumerate(KERNEL_TAPS):
        summed = summed + jnp.einsum(
            "ok,khw->ohw",
            kernel[tap_index],
            padded[:, tap_row : tap_row + height, tap_col : tap_col + breadth],
            preferred_element_type=jnp.float32,
        )
    return summed


def backward_conv(cotangent, kernel):
    height, breadth = (cotangent.shape[1], cotangent.shape[2])
    padded = jnp.pad(cotangent, ((0, 0), (1, 1), (1, 1)))
    summed = jnp.zeros((kernel.shape[2], height, breadth), jnp.float32)
    for tap_index, (tap_row, tap_col) in enumerate(KERNEL_TAPS):
        summed = summed + jnp.einsum(
            "ok,ohw->khw",
            kernel[tap_index],
            padded[:, 2 - tap_row : 2 - tap_row + height, 2 - tap_col : 2 - tap_col + breadth],
            preferred_element_type=jnp.float32,
        )
    return summed


def kernel_grad(cotangent, values):
    height, breadth = (values.shape[1], values.shape[2])
    padded = jnp.pad(values, ((0, 0), (1, 1), (1, 1)))
    pieces = [
        jnp.einsum(
            "ohw,khw->ok",
            cotangent,
            padded[:, tap_row : tap_row + height, tap_col : tap_col + breadth],
            preferred_element_type=jnp.float32,
        )
        for tap_row, tap_col in KERNEL_TAPS
    ]
    return jnp.stack(pieces)


def silu_slope(pre_act):
    sigmoid = jax.nn.sigmoid(pre_act)
    return sigmoid * (1.0 + pre_act * (1.0 - sigmoid))


def patch_pass(inputs, out_grad, kernel_in, kernel_mid, kernel_out):
    pre_one = forward_conv(inputs, kernel_in)
    hidden_one = jax.nn.silu(pre_one).astype(jnp.bfloat16)
    pre_two = forward_conv(hidden_one, kernel_mid)
    hidden_two = (hidden_one.astype(jnp.float32) + jax.nn.silu(pre_two)).astype(jnp.bfloat16)
    result = forward_conv(hidden_two, kernel_out)
    grad_two = backward_conv(out_grad, kernel_out)
    delta_two = (grad_two * silu_slope(pre_two)).astype(jnp.bfloat16)
    grad_one = grad_two + backward_conv(delta_two, kernel_mid)
    delta_one = (grad_one * silu_slope(pre_one)).astype(jnp.bfloat16)
    return (
        result,
        kernel_grad(delta_one, inputs),
        kernel_grad(delta_two, hidden_one),
        kernel_grad(out_grad, hidden_two),
    )


def run_patches(inputs, out_grads, kernel_in, kernel_mid, kernel_out):
    initial = (
        jnp.zeros(kernel_in.shape, jnp.float32),
        jnp.zeros(kernel_mid.shape, jnp.float32),
        jnp.zeros(kernel_out.shape, jnp.float32),
    )

    def step_patch(running, slot_pair):
        result, part_in, part_mid, part_out = patch_pass(
            slot_pair[0], slot_pair[1], kernel_in, kernel_mid, kernel_out
        )
        return ((running[0] + part_in, running[1] + part_mid, running[2] + part_out), result)

    return lax.scan(step_patch, initial, (inputs, out_grads))


def fold_canvas(canvas, keep_top, keep_bottom):
    extended = extended_2(canvas, (("lat", 1), ("lon", 2)), MARGIN)
    height = canvas.shape[1] - 2 * MARGIN
    breadth = canvas.shape[2] - 2 * MARGIN
    inner_rows = slice(2 * MARGIN, 2 * MARGIN + height)
    inner_cols = slice(2 * MARGIN, 2 * MARGIN + breadth)
    center_part = extended[:, inner_rows, inner_cols]
    col_left = ((0, 0), (0, 0), (0, breadth - MARGIN))
    col_right = ((0, 0), (0, 0), (breadth - MARGIN, 0))
    upper_part = (
        extended[:, :MARGIN, inner_cols]
        + jnp.pad(extended[:, :MARGIN, :MARGIN], col_left)
        + jnp.pad(extended[:, :MARGIN, -MARGIN:], col_right)
    )
    lower_part = (
        extended[:, -MARGIN:, inner_cols]
        + jnp.pad(extended[:, -MARGIN:, :MARGIN], col_left)
        + jnp.pad(extended[:, -MARGIN:, -MARGIN:], col_right)
    )
    summed = (
        center_part
        + jnp.pad(extended[:, inner_rows, :MARGIN], col_left)
        + jnp.pad(extended[:, inner_rows, -MARGIN:], col_right)
    )
    summed = summed + jnp.pad(upper_part * keep_top, ((0, 0), (0, height - MARGIN), (0, 0)))
    summed = summed + jnp.pad(lower_part * keep_bottom, ((0, 0), (height - MARGIN, 0), (0, 0)))
    return summed


def shards(
    fields, cotangent, kernel_in, kernel_mid, kernel_out, patch_anchors, blend_weights, tile_counts
):
    channels, height, breadth = (fields.shape[0], fields.shape[1], fields.shape[2])
    canvas_rows = height + 2 * MARGIN
    canvas_cols = breadth + 2 * MARGIN
    lat_size = lax.axis_size("lat")
    lat_index = lax.axis_index("lat")
    keep_top = (lat_index > 0).astype(jnp.float32)
    keep_bottom = (lat_index < lat_size - 1).astype(jnp.float32)
    slot_count = tile_counts[0, 0]
    slot_live = (jnp.arange(SLOTS) < slot_count).astype(jnp.int32)
    weights = (blend_weights * slot_live[:, None, None]).astype(jnp.float32)
    starts = patch_anchors[0, 0]

    def place_slots(per_slot):
        canvas = jnp.zeros((per_slot.shape[1], canvas_rows, canvas_cols), jnp.float32)
        for slot_index in range(SLOTS):
            corner = (jnp.int32(0), starts[slot_index, 0], starts[slot_index, 1])
            current = lax.dynamic_slice(canvas, corner, per_slot.shape[1:])
            canvas = lax.dynamic_update_slice(canvas, current + per_slot[slot_index], corner)
        return canvas

    total_weight = jnp.maximum(
        fold_canvas(place_slots(weights[:, None]), keep_top, keep_bottom), 1.0
    )
    scaled = (cotangent.astype(jnp.float32) / total_weight).astype(jnp.bfloat16)
    wide_fields, wide_scaled = (
        extended_2(fields, (("lat", 1), ("lon", 2)), MARGIN),
        extended_2(scaled, (("lat", 1), ("lon", 2)), MARGIN),
    )
    row_ids = jnp.arange(canvas_rows)[None, :, None]
    keep_rows = ((row_ids >= MARGIN) | (keep_top > 0.0)) & (
        (row_ids < height + MARGIN) | (keep_bottom > 0.0)
    )
    wide_fields = jnp.where(keep_rows, wide_fields, jnp.zeros_like(wide_fields))
    wide_scaled = jnp.where(keep_rows, wide_scaled, jnp.zeros_like(wide_scaled))
    window_list = []
    grad_list = []
    for slot_index in range(SLOTS):
        corner = (jnp.int32(0), starts[slot_index, 0], starts[slot_index, 1])
        window_list.append(lax.dynamic_slice(wide_fields, corner, (channels, height, breadth)))
        scaled_window = lax.dynamic_slice(wide_scaled, corner, (channels, height, breadth)).astype(
            jnp.float32
        )
        grad_list.append((weights[slot_index] * scaled_window).astype(jnp.bfloat16))
    inputs = jnp.stack(window_list)
    out_grads = jnp.stack(grad_list)
    half_slots = SLOTS // 2
    upper_half = (lat_index >= lat_size // 2).astype(jnp.int32)
    first_count = jnp.where(upper_half == 0, slot_count, SLOTS - slot_count)
    outgoing_inputs = jnp.where(upper_half == 0, inputs[half_slots:], inputs[:half_slots])
    outgoing_grads = jnp.where(upper_half == 0, out_grads[half_slots:], out_grads[:half_slots])
    incoming_inputs, incoming_grads = shifted(
        (outgoing_inputs, outgoing_grads), "lat", lat_size // 2
    )
    table_inputs = jnp.concatenate([inputs, incoming_inputs], axis=0)
    table_grads = jnp.concatenate([out_grads, incoming_grads], axis=0)
    position = upper_half * half_slots + jnp.arange(half_slots, dtype=jnp.int32)
    picked = jnp.where(
        position < first_count,
        jnp.where(upper_half == 0, position, position + SLOTS - half_slots),
        jnp.where(upper_half == 0, SLOTS + position - first_count, position - first_count),
    )
    picked = jnp.clip(picked, 0, SLOTS + half_slots - 1)
    totals, computed = run_patches(
        jnp.take(table_inputs, picked, axis=0),
        jnp.take(table_grads, picked, axis=0),
        kernel_in,
        kernel_mid,
        kernel_out,
    )
    returned = shifted(computed, "lat", lat_size // 2)
    ordered = jnp.where(
        upper_half == 0,
        jnp.concatenate([computed, returned], axis=0),
        jnp.concatenate([returned, computed], axis=0),
    )
    where_slot = jnp.clip(
        jnp.arange(SLOTS, dtype=jnp.int32) + upper_half * first_count, 0, SLOTS - 1
    )
    outputs = jnp.take(ordered, where_slot, axis=0)
    weighted = weights[:, None] * outputs
    numerator = fold_canvas(place_slots(weighted), keep_top, keep_bottom)
    blended = numerator / total_weight
    summed_grads = lax.psum((totals[0], totals[1], totals[2]), ("lat", "lon"))
    return (blended, summed_grads[0], summed_grads[1], summed_grads[2])


def solution(mesh):
    return jax.shard_map(
        shards,
        mesh=mesh,
        in_specs=(
            P(None, "lat", "lon"),
            P(None, "lat", "lon"),
            P(),
            P(),
            P(),
            P("lat", "lon", None, None),
            P(None, "lat", "lon"),
            P("lat", "lon"),
        ),
        out_specs=(P(None, "lat", "lon"), P(), P(), P()),
        check_vma=False,
    )
```

profile of v0, /device:TPU:1, one launch (start us, length us, event | category | flops | bytes accessed | tf_op | source)
XLA Modules:
  0.0 499.0 jit_solution(12220531734381858021)
XLA Ops:
  22.0 0.8 dynamic_update_slice.31
  22.9 0.8 dynamic_update_slice.32
  28.0 2.3 collective-permute-start
  30.3 0.8 collective-permute-start.1
  31.2 3.8 collective-permute-start.10
  35.7 6.6 %collective-permute-start.3 = (f32[1,24,4]{2,1,0:T(8,128)S(1)}, f32[1,24,4]{2,1,0:T(8,128)S(1)}, u32[]{:S(2)}, u32[]{:S(2)}) collective-permute-start(f32[1,24,4]{2,1,0:T(8,128)S(1)} %get-tuple-element.254), channel_id=1, source_target_pairs={{1,0},{2,1},{3,2},{4,3},{5,4},{6,5},{7,6},{8,7},{9,8},{10,9},{11,1... | collective-permute-start | bytes 1160 | tf_op jit(solution)/shard_map/ppermute | solution.py:22
  42.3 1.0 collective-permute-done.2
  44.9 1.1 collective-permute-start.5
  46.4 5.5 %collective-permute-start.12 = (bf16[32,16,4]{2,1,0:T(8,128)(2,1)S(1)}, bf16[32,16,4]{2,1,0:T(8,128)(2,1)S(1)}, u32[]{:S(2)}, u32[]{:S(2)}) collective-permute-start(bf16[32,16,4]{2,1,0:T(8,128)(2,1)S(1)} %get-tuple-element.246), channel_id=1, source_target_pairs={{1,0},{2,1},{3,2},{4,3},{5,4},{6,5},{7,6},{8,7},{9,8},{10,9},{11,1... | collective-permute-start | bytes 12296 | tf_op jit(solution)/shard_map/ppermute | solution.py:22
  52.2 18.8 %collective-permute-start.7 = (bf16[32,16,4]{2,1,0:T(8,128)(2,1)S(1)}, bf16[32,16,4]{2,1,0:T(8,128)(2,1)S(1)}, u32[]{:S(2)}, u32[]{:S(2)}) collective-permute-start(bf16[32,16,4]{2,1,0:T(8,128)(2,1)S(1)} %get-tuple-element.248), channel_id=1, source_target_pairs={{1,0},{2,1},{3,2},{4,3},{5,4},{6,5},{7,6},{8,7},{9,8},{10,9},{11,1... | collective-permute-start | bytes 12296 | tf_op jit(solution)/shard_map/ppermute | solution.py:22
  71.1 1.9 collective-permute-done.7
  73.0 1.0 maximum_select_fusion.2
  75.8 1.1 collective-permute-start.13
  77.0 3.1 collective-permute-done.8
  80.6 2.2 collective-permute-done.13
  83.5 0.8 broadcast_select_fusion
  84.5 72.5 %while.19 = (s32[]{:T(128)}, f32[9,128,32]{1,2,0:T(8,128)S(1)}, f32[9,128,128]{2,1,0:T(8,128)S(1)}, f32[9,32,128]{2,1,0:T(8,128)}, f32[2,32,8,256]{3,2,1,0:T(8,1...) while((s32[]{:T(128)}, f32[9,128,32]{1,2,0:T(8,128)S(1)}, ...), condition=%wide.region_1.3_spmd.clone, body=%wide.region_0.2_spmd.clone.sunk | while | flops 2583609344 | bytes 133587216 | solution.py:112
  84.5 1.0 constant_dynamic-slice_fusion.3
  88.9 1.6 multiply_convert_fusion.8
  96.9 0.8 add_convert_fusion.2
  100.2 0.8 copy-done.8
  101.2 0.8 fusion.448
  102.0 0.8 fusion.449
  102.8 0.8 fusion.450
  103.7 0.9 fusion.451
  104.5 0.8 fusion.452
  105.3 0.9 fusion.453
  106.2 0.8 fusion.454
  107.1 0.8 fusion.455
  107.9 0.8 fusion.456
  108.7 1.6 select_add_fusion.8
  116.0 0.9 copy-done.20
  119.8 0.9 copy-done.5
  120.7 1.0 constant_dynamic-slice_fusion.3
  125.1 1.6 multiply_convert_fusion.8
  133.1 0.8 add_convert_fusion.2
  136.4 0.8 copy-done.8
  137.4 0.8 fusion.448
  138.2 0.8 fusion.449
  139.0 0.8 fusion.450
  139.9 0.9 fusion.451
  140.8 0.8 fusion.452
  141.6 0.9 fusion.453
  142.4 0.8 fusion.454
  143.3 0.8 fusion.455
  144.1 0.8 fusion.456
  144.9 1.7 select_add_fusion.8
  152.3 0.9 copy-done.20
  156.1 0.9 copy-done.5
  157.5 7.7 %collective-permute-done.14 = f32[2,32,8,256]{3,2,1,0:T(8,128)S(1)} collective-permute-done((f32[2,32,8,256]{3,2,1,0:T(8,128)}, f32[2,32,8,256]{3,2,1,0:T(8,128)S(1)}, u32[]{:S(2)}, u32[]{:S(2)}) %collective-permute-start.14) | collective-permute-done | bytes 524320 | tf_op jit(solution)/shard_map/ppermute | solution.py:30
  165.2 1.3 maximum_select_fusion
  167.6 10.2 %dynamic_update_slice.35 = f32[32,16,264]{2,1,0:T(8,128)S(1)} dynamic-update-slice(f32[32,16,264]{2,1,0:T(8,128)S(1)} %broadcast_in_dim.59, f32[32,8,256]{2,1,0:T(8,128)S(1)} %slice_bitcast_fusion.3, s32[]{:T(128)} %constant.84.clone.1, s32[]{:T(128)S(6)} %select_n.136, s32[]{:T(128)S(6)} %select_n.137) | dynamic-update-slice | bytes 524292 | tf_op jit(solution)/shard_map/dynamic_update_slice | solution.py:164
  177.9 10.2 %dynamic_update_slice.36 = f32[32,16,264]{2,1,0:T(8,128)S(1)} dynamic-update-slice(f32[32,16,264]{2,1,0:T(8,128)S(1)} %dynamic_update_slice.35, f32[32,8,256]{2,1,0:T(8,128)S(1)} %fusion.200, s32[]{:T(128)} %constant.84.clone.1, s32[]{:T(128)S(6)} %select_n.138, s32[]{:T(128)S(6)} %select_n.139) | dynamic-update-slice | bytes 524292 | tf_op jit(solution)/shard_map/dynamic_update_slice | solution.py:164
  188.2 10.1 %dynamic_update_slice.37 = f32[32,16,264]{2,1,0:T(8,128)S(1)} dynamic-update-slice(f32[32,16,264]{2,1,0:T(8,128)S(1)} %dynamic_update_slice.36, f32[32,8,256]{2,1,0:T(8,128)S(1)} %fusion.199, s32[]{:T(128)} %constant.84.clone.1, s32[]{:T(128)S(6)} %select_n.140, s32[]{:T(128)S(6)} %select_n.141) | dynamic-update-slice | bytes 524292 | tf_op jit(solution)/shard_map/dynamic_update_slice | solution.py:164
  198.5 10.1 %dynamic_update_slice.38 = f32[32,16,264]{2,1,0:T(8,128)S(1)} dynamic-update-slice(f32[32,16,264]{2,1,0:T(8,128)S(1)} %dynamic_update_slice.37, f32[32,8,256]{2,1,0:T(8,128)S(1)} %fusion.198, s32[]{:T(128)} %constant.84.clone.1, s32[]{:T(128)S(6)} %select_n.142, s32[]{:T(128)S(6)} %select_n.143) | dynamic-update-slice | bytes 524292 | tf_op jit(solution)/shard_map/dynamic_update_slice | solution.py:164
  209.5 2.6 collective-permute-done.15
  212.1 2.5 collective-permute-done.16
  214.8 7.4 %collective-permute-start.17 = (f32[32,24,4]{2,1,0:T(8,128)S(1)}, f32[32,24,4]{2,1,0:T(8,128)S(1)}, u32[]{:S(2)}, u32[]{:S(2)}) collective-permute-start(f32[32,24,4]{2,1,0:T(8,128)S(1)} %get-tuple-element.237), channel_id=1, source_target_pairs={{0,1},{1,2},{2,3},{3,4},{4,5},{5,6},{6,7},{7,8},{8,9},{9,10},{10,1... | collective-permute-start | bytes 36872 | tf_op jit(solution)/shard_map/ppermute | solution.py:19
  222.2 7.6 %collective-permute-start.18 = (f32[32,24,4]{2,1,0:T(8,128)S(1)}, f32[32,24,4]{2,1,0:T(8,128)S(1)}, u32[]{:S(2)}, u32[]{:S(2)}) collective-permute-start(f32[32,24,4]{2,1,0:T(8,128)S(1)} %get-tuple-element.238), channel_id=1, source_target_pairs={{1,0},{2,1},{3,2},{4,3},{5,4},{6,5},{7,6},{8,7},{9,8},{10,9},{11,1... | collective-permute-start | bytes 36872 | tf_op jit(solution)/shard_map/ppermute | solution.py:22
  229.8 5.1 %collective-permute-done.17 = f32[32,24,4]{2,1,0:T(8,128)S(1)} collective-permute-done((f32[32,24,4]{2,1,0:T(8,128)S(1)}, f32[32,24,4]{2,1,0:T(8,128)S(1)}, u32[]{:S(2)}, u32[]{:S(2)}) %collective-permute-start.17) | collective-permute-done | bytes 12320 | tf_op jit(solution)/shard_map/ppermute | solution.py:19
  237.5 0.9 fusion.197
  238.4 249.2 %all-reduce.24.cloned.1.call-done = (f32[9,128,32]{1,2,0:T(8,128)}, f32[9,128,128]{2,1,0:T(8,128)}, f32[9,32,128]{2,1,0:T(8,128)}) async-done(((f32[9,128,32]{1,2,0:T(8,128)}, f32[9,128,128]{2,1,0:T(8,128)}, f32[9,32,128]{2,1,0:T(8,128)}), (f32[9,128,32]{1,2,0:T(8,128)}, f32[9,128,128]{2,1,0:T(8,128)}, f32[9,32,128]{2,1,0:T(8,128)})) %all-reduce.24.cloned.1.call-update) | async-done | bytes 884752 | tf_op jit(solution)/shard_map/psum | solution.py:229
  487.6 1.6 copy.283
  489.2 2.0 copy.284
  (267 shorter events, 57.2 us)
Async XLA Ops:
  7.2 0.7 copy-start.19
  7.2 480.4 %all-reduce.24.cloned.1.call-start = ((), (), s32[]{:S(2)}) async-start(), calls=%async_computation | async-start | bytes 1769472 | tf_op jit(solution)/shard_map/psum | solution.py:229
  8.5 10.9 %copy-start.18 = (s32[4,8,256]{2,1,0:T(8,128)S(1)}, s32[4,8,256]{2,1,0:T(8,128)}, u32[]{:S(2)}) copy-start(s32[4,8,256]{2,1,0:T(8,128)} %param.18) | copy-start | bytes 98308
  19.4 7.7 %copy-start.12 = (f32[4,8,256]{2,1,0:T(8,128)}, f32[4,8,256]{2,1,0:T(8,128)S(1)}, u32[]{:S(2)}) copy-start(f32[4,8,256]{2,1,0:T(8,128)S(1)} %multiply_convert_fusion.6) | copy-start | bytes 98308
  22.0 9.1 %copy-start.7 = (bf16[32,8,256]{2,1,0:T(8,128)(2,1)S(1)}, bf16[32,8,256]{2,1,0:T(8,128)(2,1)}, u32[]{:S(2)}) copy-start(bf16[32,8,256]{2,1,0:T(8,128)(2,1)} %param.12) | copy-start | bytes 393220
  28.0 7.0 %collective-permute-start = (f32[1,4,264]{2,1,0:T(4,128)S(1)}, f32[1,4,264]{2,1,0:T(4,128)S(1)}, u32[]{:S(2)}, u32[]{:S(2)}) collective-permute-start(f32[1,4,264]{2,1,0:T(4,128)S(1)} %get-tuple-element.260), channel_id=1, source_target_pairs={{0,16},{16,32},{32,48},{48,64},{64,80},{80,96},{96,112},{112,128},... | collective-permute-start | bytes 12680 | tf_op jit(solution)/shard_map/ppermute | solution.py:19
  30.3 4.7 collective-permute-start.1
  31.2 12.4 %copy-start.15 = (bf16[32,8,256]{2,1,0:T(8,128)(2,1)S(1)}, bf16[32,8,256]{2,1,0:T(8,128)(2,1)}, u32[]{:S(2)}) copy-start(bf16[32,8,256]{2,1,0:T(8,128)(2,1)} %param.13) | copy-start | bytes 393220
  31.2 14.8 %collective-permute-start.10 = (bf16[32,4,256]{2,1,0:T(4,128)(2,1)S(1)}, bf16[32,4,256]{2,1,0:T(4,128)(2,1)S(1)}, u32[]{:S(2)}, u32[]{:S(2)}) collective-permute-start(bf16[32,4,256]{2,1,0:T(4,128)(2,1)S(1)} %get-tuple-element.250), channel_id=1, source_target_pairs={{16,0},{32,16},{48,32},{64,48},{80,64},{96,80},{112,96},{128,112},... | collective-permute-start | bytes 196616 | tf_op jit(solution)/shard_map/ppermute | solution.py:22
  35.0 11.0 %collective-permute-start.9 = (bf16[32,4,256]{2,1,0:T(4,128)(2,1)S(1)}, bf16[32,4,256]{2,1,0:T(4,128)(2,1)S(1)}, u32[]{:S(2)}, u32[]{:S(2)}) collective-permute-start(bf16[32,4,256]{2,1,0:T(4,128)(2,1)S(1)} %get-tuple-element.249), channel_id=1, source_target_pairs={{0,16},{16,32},{32,48},{48,64},{64,80},{80,96},{96,112},{112,128},... | collective-permute-start | bytes 196616 | tf_op jit(solution)/shard_map/ppermute | solution.py:19
  35.1 8.2 %collective-permute-start.2 = (f32[1,24,4]{2,1,0:T(8,128)S(1)}, f32[1,24,4]{2,1,0:T(8,128)S(1)}, u32[]{:S(2)}, u32[]{:S(2)}) collective-permute-start(f32[1,24,4]{2,1,0:T(8,128)S(1)} %get-tuple-element.253), channel_id=1, source_target_pairs={{0,1},{1,2},{2,3},{3,4},{4,5},{5,6},{6,7},{7,8},{8,9},{9,10},{10,1... | collective-permute-start | bytes 1160 | tf_op jit(solution)/shard_map/ppermute | solution.py:19
  35.7 7.6 %collective-permute-start.3 = (f32[1,24,4]{2,1,0:T(8,128)S(1)}, f32[1,24,4]{2,1,0:T(8,128)S(1)}, u32[]{:S(2)}, u32[]{:S(2)}) collective-permute-start(f32[1,24,4]{2,1,0:T(8,128)S(1)} %get-tuple-element.254), channel_id=1, source_target_pairs={{1,0},{2,1},{3,2},{4,3},{5,4},{6,5},{7,6},{8,7},{9,8},{10,9},{11,1... | collective-permute-start | bytes 1160 | tf_op jit(solution)/shard_map/ppermute | solution.py:22
  43.6 0.6 copy-start.16
  44.2 7.7 %collective-permute-start.4 = (bf16[32,4,256]{2,1,0:T(4,128)(2,1)S(1)}, bf16[32,4,256]{2,1,0:T(4,128)(2,1)S(1)}, u32[]{:S(2)}, u32[]{:S(2)}) collective-permute-start(bf16[32,4,256]{2,1,0:T(4,128)(2,1)S(1)} %get-tuple-element.251), channel_id=1, source_target_pairs={{0,16},{16,32},{32,48},{48,64},{64,80},{80,96},{96,112},{112,128},... | collective-permute-start | bytes 196616 | tf_op jit(solution)/shard_map/ppermute | solution.py:19
  44.9 7.0 %collective-permute-start.5 = (bf16[32,4,256]{2,1,0:T(4,128)(2,1)S(1)}, bf16[32,4,256]{2,1,0:T(4,128)(2,1)S(1)}, u32[]{:S(2)}, u32[]{:S(2)}) collective-permute-start(bf16[32,4,256]{2,1,0:T(4,128)(2,1)S(1)} %get-tuple-element.252), channel_id=1, source_target_pairs={{16,0},{32,16},{48,32},{64,48},{80,64},{96,80},{112,96},{128,112},... | collective-permute-start | bytes 196616 | tf_op jit(solution)/shard_map/ppermute | solution.py:22
  46.3 24.8 %collective-permute-start.11 = (bf16[32,16,4]{2,1,0:T(8,128)(2,1)S(1)}, bf16[32,16,4]{2,1,0:T(8,128)(2,1)S(1)}, u32[]{:S(2)}, u32[]{:S(2)}) collective-permute-start(bf16[32,16,4]{2,1,0:T(8,128)(2,1)S(1)} %get-tuple-element.245), channel_id=1, source_target_pairs={{0,1},{1,2},{2,3},{3,4},{4,5},{5,6},{6,7},{7,8},{8,9},{9,10},{10,1... | collective-permute-start | bytes 12296 | tf_op jit(solution)/shard_map/ppermute | solution.py:19
  46.4 24.7 %collective-permute-start.12 = (bf16[32,16,4]{2,1,0:T(8,128)(2,1)S(1)}, bf16[32,16,4]{2,1,0:T(8,128)(2,1)S(1)}, u32[]{:S(2)}, u32[]{:S(2)}) collective-permute-start(bf16[32,16,4]{2,1,0:T(8,128)(2,1)S(1)} %get-tuple-element.246), channel_id=1, source_target_pairs={{1,0},{2,1},{3,2},{4,3},{5,4},{6,5},{7,6},{8,7},{9,8},{10,9},{11,1... | collective-permute-start | bytes 12296 | tf_op jit(solution)/shard_map/ppermute | solution.py:22
  52.1 18.9 %collective-permute-start.6 = (bf16[32,16,4]{2,1,0:T(8,128)(2,1)S(1)}, bf16[32,16,4]{2,1,0:T(8,128)(2,1)S(1)}, u32[]{:S(2)}, u32[]{:S(2)}) collective-permute-start(bf16[32,16,4]{2,1,0:T(8,128)(2,1)S(1)} %get-tuple-element.247), channel_id=1, source_target_pairs={{0,1},{1,2},{2,3},{3,4},{4,5},{5,6},{6,7},{7,8},{8,9},{9,10},{10,1... | collective-permute-start | bytes 12296 | tf_op jit(solution)/shard_map/ppermute | solution.py:19
  52.2 20.8 %collective-permute-start.7 = (bf16[32,16,4]{2,1,0:T(8,128)(2,1)S(1)}, bf16[32,16,4]{2,1,0:T(8,128)(2,1)S(1)}, u32[]{:S(2)}, u32[]{:S(2)}) collective-permute-start(bf16[32,16,4]{2,1,0:T(8,128)(2,1)S(1)} %get-tuple-element.248), channel_id=1, source_target_pairs={{1,0},{2,1},{3,2},{4,3},{5,4},{6,5},{7,6},{8,7},{9,8},{10,9},{11,1... | collective-permute-start | bytes 12296 | tf_op jit(solution)/shard_map/ppermute | solution.py:22
  74.7 5.3 %collective-permute-start.8 = (bf16[2,32,8,256]{3,2,1,0:T(8,128)(2,1)S(1)}, bf16[2,32,8,256]{3,2,1,0:T(8,128)(2,1)S(1)}, u32[]{:S(2)}, u32[]{:S(2)}) collective-permute-start(bf16[2,32,8,256]{3,2,1,0:T(8,128)(2,1)S(1)} %maximum_select_fusion.3), channel_id=1, source_target_pairs={{0,128},{16,144},{32,160},{48,176},{64,192},{80,208},{96,224},{112... | collective-permute-start | bytes 786440 | tf_op jit(solution)/shard_map/ppermute | solution.py:30
  75.8 7.0 %collective-permute-start.13 = (bf16[2,32,8,256]{3,2,1,0:T(8,128)(2,1)S(1)}, bf16[2,32,8,256]{3,2,1,0:T(8,128)(2,1)S(1)}, u32[]{:S(2)}, u32[]{:S(2)}) collective-permute-start(bf16[2,32,8,256]{3,2,1,0:T(8,128)(2,1)S(1)} %maximum_select_fusion.4), channel_id=1, source_target_pairs={{0,128},{16,144},{32,160},{48,176},{64,192},{80,208},{96,224},{112... | collective-permute-start | bytes 786440 | tf_op jit(solution)/shard_map/ppermute | solution.py:30
  83.5 1.0 copy-start
  83.5 1.0 copy-start.2
  83.5 1.0 copy-start.6
  84.5 1.0 copy-start.4
  99.9 1.0 copy-start.8
  101.2 4.2 copy-start.9
  115.7 1.2 copy-start.20
  119.7 1.0 copy-start.5
  120.7 1.0 copy-start.4
  136.2 1.0 copy-start.8
  137.4 4.2 copy-start.9
  152.0 1.2 copy-start.20
  156.0 1.0 copy-start.5
  157.0 9.6 %copy-start.1 = (f32[9,128,128]{2,1,0:T(8,128)}, f32[9,128,128]{2,1,0:T(8,128)S(1)}, u32[]{:S(2)}) copy-start(f32[9,128,128]{2,1,0:T(8,128)S(1)} %get-tuple-element.135) | copy-start | bytes 1769476
  157.0 9.6 %copy-start.3 = (f32[9,128,32]{1,2,0:T(8,128)}, f32[9,128,32]{1,2,0:T(8,128)S(1)}, u32[]{:S(2)}) copy-start(f32[9,128,32]{1,2,0:T(8,128)S(1)} %get-tuple-element.134) | copy-start | bytes 442372
  157.0 8.2 %collective-permute-start.14 = (f32[2,32,8,256]{3,2,1,0:T(8,128)}, f32[2,32,8,256]{3,2,1,0:T(8,128)S(1)}, u32[]{:S(2)}, u32[]{:S(2)}) collective-permute-start(f32[2,32,8,256]{3,2,1,0:T(8,128)} %get-tuple-element.133), channel_id=1, source_target_pairs={{0,128},{16,144},{32,160},{48,176},{64,192},{80,208},{96,224},{112... | collective-permute-start | bytes 1572872 | tf_op jit(solution)/shard_map/ppermute | solution.py:30
  166.6 0.8 copy-start.13
  208.7 3.4 collective-permute-start.15
  209.5 5.1 %collective-permute-start.16 = (f32[32,4,264]{2,1,0:T(4,128)S(1)}, f32[32,4,264]{2,1,0:T(4,128)S(1)}, u32[]{:S(2)}, u32[]{:S(2)}) collective-permute-start(f32[32,4,264]{2,1,0:T(4,128)S(1)} %get-tuple-element.240), channel_id=1, source_target_pairs={{16,0},{32,16},{48,32},{64,48},{80,64},{96,80},{112,96},{128,112},... | collective-permute-start | bytes 405512 | tf_op jit(solution)/shard_map/ppermute | solution.py:22
  214.8 20.0 %collective-permute-start.17 = (f32[32,24,4]{2,1,0:T(8,128)S(1)}, f32[32,24,4]{2,1,0:T(8,128)S(1)}, u32[]{:S(2)}, u32[]{:S(2)}) collective-permute-start(f32[32,24,4]{2,1,0:T(8,128)S(1)} %get-tuple-element.237), channel_id=1, source_target_pairs={{0,1},{1,2},{2,3},{3,4},{4,5},{5,6},{6,7},{7,8},{8,9},{9,10},{10,1... | collective-permute-start | bytes 36872 | tf_op jit(solution)/shard_map/ppermute | solution.py:19
  222.2 13.4 %collective-permute-start.18 = (f32[32,24,4]{2,1,0:T(8,128)S(1)}, f32[32,24,4]{2,1,0:T(8,128)S(1)}, u32[]{:S(2)}, u32[]{:S(2)}) collective-permute-start(f32[32,24,4]{2,1,0:T(8,128)S(1)} %get-tuple-element.238), channel_id=1, source_target_pairs={{1,0},{2,1},{3,2},{4,3},{5,4},{6,5},{7,6},{8,7},{9,8},{10,9},{11,1... | collective-permute-start | bytes 36872 | tf_op jit(solution)/shard_map/ppermute | solution.py:22
  234.8 0.8 copy-start.10
  235.6 0.7 copy-start.11
  236.5 0.9 slice-start
  236.5 1.0 slice-start.1
  236.5 1.0 copy-start.17
  489.2 2.0 copy-start.14
Sparse Core Ops, SparseCore 0:
  222.3 265.1 all-reduce.23
where the time goes:
time: 508 us; the launch traced here: 499 us
  waiting for transfers between devices  275 us (54%)
  local copies, waits for them, and re-layouts  62.7 us (12%)
  matrix products  60.3 us (12%)
  starting transfers between devices  58.3 us (11%)
  between operations  30.9 us (6%)
  other arithmetic  10.7 us (2%)
    psum x1, waiting for transfers between devices, shards(): summed_grads = lax.psum((totals[0], totals[1], totals[2]), ('lat', 'lon'))  249 us
    ppermute x8, starting transfers between devices, extended_2(): lax.ppermute(lax.slice_in_dim(block, 0, width, axis=dim), axis, backward)  44.2 us
    dynamic_update_slice x8, local copies, waits for them, and re-layouts, place_slots(): lax.dynamic_update_slice(canvas, current + per_slot[slot_index], corner)  43.7 us
    dot_general x54, matrix products, kernel_grad(): jnp.einsum('ohw,khw->ok', cotangent, padded[:, tap_row:tap_row + height,...  25.4 us
    dot_general x54, matrix products, forward_conv(): jnp.einsum('ok,khw->ohw', kernel[tap_index], padded[:, tap_row:tap_row +...  21.3 us
    dot_general x36, matrix products, backward_conv(): jnp.einsum('ok,ohw->khw', kernel[tap_index], padded[:, 2 - tap_row:2 - ta...  13.6 us
    ppermute x3, waiting for transfers between devices, shifted(): return lax.ppermute(value, axis, pairs)  13 us
    ppermute x8, starting transfers between devices, extended_2(): lax.ppermute(lax.slice_in_dim(block, block.shape[dim] - width, None, axis...  11.9 us
  transfers between devices with their start and end apart: 20, of which 9 were waited for; matrix products, arithmetic and copies ran while one was open for 1% of the time, Pallas kernels for 0%

commit v1 on v0

v1 whole, which is shorter than its diff:
```python
import functools

import jax
import jax.numpy as jnp
from jax import lax
from jax.experimental import pallas as pl
from jax.experimental.pallas import tpu as pltpu
from jax.sharding import PartitionSpec as P

MESH = pl.DeviceIdType.MESH
F32 = jnp.float32
BF16 = jnp.bfloat16

CH = 32
WD = 128
TR = 8
TC = 256
MG = 4
SLOTS = 4
EXT = 384
CELLS = TR * TC
PAD = (TR + 2) * TC

NB = ((-1, 0), (1, 0), (0, -1), (0, 1), (-1, -1), (-1, 1), (1, -1), (1, 1))
UP, DN, LF, RT, UL, UR, DL, DR = range(8)

G_MID, G_OUT, G_IN, G_END = 0, 9 * WD, 9 * WD + 9 * CH, 9 * WD + 18 * CH


def vmem(n):
    return [pl.BlockSpec(memory_space=pltpu.VMEM)] * n


def smem(n):
    return [pl.BlockSpec(memory_space=pltpu.SMEM)] * n


def lanes_of(shape):
    return lax.broadcasted_iota(jnp.int32, shape, len(shape) - 1)


def prep_kernel(anch, cnt, f_ref, c_ref, w_ref, fc_ref, e_ref, cv_ref, scr):
    for half in range(2):
        at = slice(half * 128, half * 128 + 128)
        scr[half] = f_ref[:, :, at].astype(F32).reshape(CH * TR, 128)
        scr[2 + half] = c_ref[:, :, at].astype(F32).reshape(CH * TR, 128)
    lane = lanes_of((2 * CH, 128))
    edge = jnp.zeros((2 * CH, 128), F32)
    for r in range(TR):
        piece = [scr[k, pl.ds(r, CH, stride=TR), :] for k in range(4)]
        row = jnp.concatenate(
            [jnp.concatenate(piece[:2], axis=1), jnp.concatenate(piece[2:], axis=1)], axis=0
        )
        fc_ref[r] = row.astype(BF16)
        first = pltpu.roll(row[:, :128], MG * r, 1) if r else row[:, :128]
        edge = jnp.where((lane >= MG * r) & (lane < MG * (r + 1)), first, edge)
        at = 32 + MG * r
        last = pltpu.roll(row[:, 128:], (at - (128 - MG)) % 128, 1)
        edge = jnp.where((lane >= at) & (lane < at + MG), last, edge)
    e_ref[...] = edge.astype(BF16)
    total = jnp.zeros((2 * TR, EXT), F32)
    for q in range(SLOTS):
        live = jnp.where(q < cnt[0, 0], 1.0, 0.0).astype(F32)
        w = w_ref[q].astype(F32) * live
        w = jnp.concatenate([w, jnp.zeros((TR, 128), F32)], axis=1)
        w = pltpu.roll(w, lax.rem(anch[q, 1] + (EXT - MG), EXT), 1)
        w = jnp.concatenate([w, jnp.zeros((TR, EXT), F32)], axis=0)
        total = total + pltpu.roll(w, anch[q, 0], 0)
    cv_ref[...] = total.astype(BF16)


def exchange_kernel(sizes, fc_ref, e_ref, cv_ref, up_ref, dn_ref, en_ref, cn_ref, ssem, rsem):
    la, lo = lax.axis_index("lat"), lax.axis_index("lon")
    nla, nlo = sizes
    where = [(lax.rem(la + di + nla, nla), lax.rem(lo + dj + nlo, nlo)) for di, dj in NB]
    barrier = pltpu.get_barrier_semaphore()
    for dev in where:
        pl.semaphore_signal(barrier, inc=1, device_id=dev, device_id_type=MESH)
    pl.semaphore_wait(barrier, len(NB))
    copies = []

    def send(src, dst, dev, k):
        copy = pltpu.make_async_remote_copy(
            src_ref=src, dst_ref=dst, send_sem=ssem.at[k], recv_sem=rsem.at[k],
            device_id=dev, device_id_type=MESH,
        )
        copy.start()
        copies.append(copy)

    send(fc_ref.at[0:MG], dn_ref, where[UP], 0)
    send(fc_ref.at[MG:TR], up_ref, where[DN], 1)
    for k, (di, dj) in enumerate(NB):
        back = NB.index((-di, -dj))
        send(cv_ref, cn_ref.at[back], where[k], 2 + back)
        if dj:
            send(e_ref, en_ref.at[back - 2], where[k], 10 + back - 2)
    for copy in copies:
        copy.wait()


def shift_cols(x, step):
    lane = lanes_of(x.shape)
    if step < 0:
        return jnp.where(lane == 0, 0.0, pltpu.roll(x, 1, 1))
    return jnp.where(lane == x.shape[1] - 1, 0.0, pltpu.roll(x, x.shape[1] - 1, 1))


def put_shifted(buf, r, x, ch):
    at = pl.multiple_of((r + 1) * TC, TC)
    buf[0:ch, pl.ds(at, TC)] = shift_cols(x, -1).astype(BF16)
    buf[ch : 2 * ch, pl.ds(at, TC)] = x.astype(BF16)
    buf[2 * ch : 3 * ch, pl.ds(at, TC)] = shift_cols(x, 1).astype(BF16)


def stacked(buf, r):
    return jnp.concatenate(
        [buf[:, pl.ds(pl.multiple_of((r + dy) * TC, TC), TC)] for dy in range(3)], axis=0
    )


def dot(a, b):
    return jnp.dot(a, b, preferred_element_type=F32)


def dot_t(a, b):
    return lax.dot_general(a, b, (((1,), (1,)), ((), ())), preferred_element_type=F32)


def patch_kernel(
    anch, cnt, fc_ref, up_ref, dn_ref, en_ref, cv_ref, cn_ref, w_ref, win_ref, wmid_ref, wout_ref,
    woutt_ref, wmidt_ref, num_ref, top_ref, bot_ref, np_ref, g_ref, inv_ref,
    ext, inv, xpb, dpb, h1b, dzb, h1, h2, sl1, sl2, dh2, dz1, oq, canvas, gmid, gout, gin,
):
    la, nla = lax.axis_index("lat"), lax.axis_size("lat")
    keep_top = la > 0
    keep_bot = la < nla - 1

    lane = lanes_of((2 * TR, EXT))
    den = cv_ref[...].astype(F32)

    def rows_of(k, canv):
        di = NB[k][0]
        zero = jnp.zeros((TR, EXT), F32)
        if di < 0:
            part = jnp.where(keep_top, canv[TR:], zero)
            return jnp.concatenate([part, zero], axis=0)
        if di > 0:
            part = jnp.where(keep_bot, canv[:TR], zero)
            return jnp.concatenate([zero, part], axis=0)
        return canv

    for k, (di, dj) in enumerate(NB):
        canv = cn_ref[k].astype(F32)
        if dj > 0:
            canv = jnp.concatenate([canv[:, 128:], canv[:, :128]], axis=1)
            canv = jnp.where((lane >= TC - MG) & (lane < TC + MG), canv, 0.0)
        if dj < 0:
            canv = jnp.concatenate([canv[:, 256:], canv[:, :256]], axis=1)
            canv = jnp.where((lane >= EXT - MG) | (lane < MG), canv, 0.0)
        den = den + rows_of(k, canv)
    inv[...] = 1.0 / jnp.maximum(den, 1.0)
    inv_ref[...] = inv[MG : MG + TR, :TC]

    hl = lanes_of((2 * CH, 128))
    for t in range(2 * TR):
        if t < MG:
            center, left, right, r, keep = up_ref[t], UL, UR, t + MG, keep_top
        elif t < MG + TR:
            center, left, right, r, keep = fc_ref[t - MG], LF, RT, t - MG, None
        else:
            center, left, right, r, keep = dn_ref[t - MG - TR], DL, DR, t - MG - TR, keep_bot
        lp = pltpu.roll(en_ref[left - 2].astype(F32), (96 - MG - MG * r) % 128, 1)
        rp = en_ref[right - 2].astype(F32)
        rp = pltpu.roll(rp, 128 - MG * r, 1) if r else rp
        row = jnp.concatenate([center.astype(F32), jnp.where(hl < 64, rp, lp)], axis=1)
        if keep is not None:
            row = jnp.where(keep, row, 0.0)
        ext[t, 0:CH, :] = row[:CH].astype(BF16)
        ext[t, CH:, :] = (row[CH:] * inv[t : t + 1, :]).astype(BF16)

    for buf in (xpb, dpb, h1b, dzb):
        z = jnp.zeros((buf.shape[0], TC), BF16)
        buf[:, 0:TC] = z
        buf[:, PAD - TC : PAD] = z
    canvas[...] = jnp.zeros_like(canvas)
    gmid[...] = jnp.zeros_like(gmid)
    gout[...] = jnp.zeros_like(gout)
    gin[...] = jnp.zeros_like(gin)

    def one_patch(q, carry):
        a, b = anch[q, 0], anch[q, 1]
        turn = lax.rem(EXT + MG - b, EXT)

        def window(r, c):
            x = pltpu.roll(ext[a + r].astype(F32), turn, 1)[:, :TC]
            pw = w_ref[q, pl.ds(r, 1), :].astype(F32)
            put_shifted(xpb, r, x[:CH], CH)
            put_shifted(dpb, r, x[CH:] * pw, CH)
            return c

        lax.fori_loop(0, TR, window, 0)

        def first(r, c):
            at = pl.ds(pl.multiple_of(r * TC, TC), TC)
            z = dot(win_ref[...], stacked(xpb, r))
            s = 0.5 + 0.5 * jnp.tanh(0.5 * z)
            h = z * s
            h1[:, at] = h.astype(BF16)
            put_shifted(h1b, r, h, WD)
            sl1[:, at] = s * (1.0 + z * (1.0 - s))
            return c

        lax.fori_loop(0, TR, first, 0)

        oq[...] = jnp.zeros_like(oq)

        def second(r, c):
            at = pl.ds(pl.multiple_of(r * TC, TC), TC)
            z = dot(wmid_ref[...], stacked(h1b, r))
            s = 0.5 + 0.5 * jnp.tanh(0.5 * z)
            h = (h1[:, at].astype(F32) + z * s).astype(BF16)
            h2[:, at] = h
            slope = s * (1.0 + z * (1.0 - s))
            p = dot(wout_ref[...], h)
            for dy in range(3):
                oq[r + 2 - dy] += p[dy * 96 : (dy + 1) * 96]
            g = dot(woutt_ref[...], stacked(dpb, r))
            dh2[:, at] = g
            put_shifted(dzb, r, g * slope, WD)
            return c

        lax.fori_loop(0, TR, second, 0)

        place = lax.rem(b + (EXT - MG), EXT)

        def blend(r, c):
            v = oq[r + 1]
            o = shift_cols(v[0:CH], -1) + v[CH : 2 * CH] + shift_cols(v[2 * CH :], 1)
            o = o * w_ref[q, pl.ds(r, 1), :].astype(F32)
            o = jnp.concatenate([o, jnp.zeros((CH, 128), F32)], axis=1)
            canvas[a + r] += pltpu.roll(o, place, 1)
            return c

        lax.fori_loop(0, TR, blend, 0)

        def third(r, c):
            at = pl.ds(pl.multiple_of(r * TC, TC), TC)
            g = dh2[:, at] + dot(wmidt_ref[...], stacked(dzb, r))
            dz1[:, at] = (g * sl1[:, at]).astype(BF16)
            return c

        lax.fori_loop(0, TR, third, 0)

        hh = h2[...]
        for dy in range(3):
            gout[dy] += dot_t(dpb[:, (2 - dy) * TC : (2 - dy) * TC + CELLS], hh)
        d1 = dz1[...]
        for dy in range(3):
            gin[dy] += dot_t(xpb[:, dy * TC : dy * TC + CELLS], d1)
        d2 = dzb[WD : 2 * WD, TC : TC + CELLS]
        for dy in range(3):
            gmid[:, dy * 384 : (dy + 1) * 384] += dot_t(d2, h1b[:, dy * TC : dy * TC + CELLS])
        return carry

    lax.fori_loop(0, cnt[0, 0], one_patch, 0)

    for r in range(TR):
        num_ref[r] = canvas[MG + r, :, :TC]
    for r in range(MG):
        top_ref[r] = canvas[r, :, :TC].astype(BF16)
        bot_ref[r] = canvas[MG + TR + r, :, :TC].astype(BF16)
    pk_lane = lanes_of((CH, 128))
    pk = jnp.zeros((CH, 128), F32)
    for t in range(2 * TR):
        v = canvas[t, :, TC:]
        hi = pltpu.roll(v, MG * t, 1) if t else v
        pk = jnp.where((pk_lane >= MG * t) & (pk_lane < MG * (t + 1)), hi, pk)
        at = 64 + MG * t
        lo = pltpu.roll(v, (at - (128 - MG)) % 128, 1)
        pk = jnp.where((pk_lane >= at) & (pk_lane < at + MG), lo, pk)
    np_ref[...] = pk.astype(BF16)
    for tap in range(9):
        g_ref[G_MID + tap * WD : G_MID + (tap + 1) * WD] = gmid[:, tap * WD : (tap + 1) * WD].astype(BF16)
        dy, dx = divmod(tap, 3)
        s = 2 - dx
        g_ref[G_OUT + tap * CH : G_OUT + (tap + 1) * CH] = gout[dy, s * CH : (s + 1) * CH].astype(BF16)
        g_ref[G_IN + tap * CH : G_IN + (tap + 1) * CH] = gin[dy, dx * CH : (dx + 1) * CH].astype(BF16)
    if g_ref.shape[0] > G_END:
        g_ref[G_END:] = jnp.zeros((g_ref.shape[0] - G_END, WD), BF16)


def reduce_kernel(
    sizes, parts, top_ref, bot_ref, np_ref, g_ref, nu_ref, nd_ref, n6_ref, gs_ref,
    buf1, buf2, mid, own, fin, ssem, rsem, s1, r1, s2, r2, s3, r3, s4, r4,
):
    la, lo = lax.axis_index("lat"), lax.axis_index("lon")
    nla, nlo = sizes
    pp = own.shape[0]
    where = [(lax.rem(la + di + nla, nla), lax.rem(lo + dj + nlo, nlo)) for di, dj in NB]
    lat_at = lambda k: lax.rem(la + k, nla)
    lon_at = lambda k: lax.rem(lo + k, nlo)
    barrier = pltpu.get_barrier_semaphore()
    for dev in where:
        pl.semaphore_signal(barrier, inc=1, device_id=dev, device_id_type=MESH)
    for k in range(1, nla):
        pl.semaphore_signal(barrier, inc=1, device_id=(lat_at(k), lo), device_id_type=MESH)
    for k in range(1, nlo):
        pl.semaphore_signal(barrier, inc=1, device_id=(la, lon_at(k)), device_id_type=MESH)
    pl.semaphore_wait(barrier, len(NB) + nla - 1 + nlo - 1)

    def copy_to(src, dst, ss, rs, dev):
        return pltpu.make_async_remote_copy(
            src_ref=src, dst_ref=dst, send_sem=ss, recv_sem=rs, device_id=dev, device_id_type=MESH
        )

    first = []
    for k in range(1, nla):
        to = lat_at(k)
        first.append(copy_to(g_ref.at[to], buf1.at[nla - k], s1.at[k], r1.at[nla - k], (to, lo)))
    for c in first:
        c.start()
    edges = [
        copy_to(top_ref, nd_ref, ssem.at[0], rsem.at[0], where[UP]),
        copy_to(bot_ref, nu_ref, ssem.at[1], rsem.at[1], where[DN]),
    ]
    for k, (di, dj) in enumerate(NB):
        if dj:
            back = NB.index((-di, -dj)) - 2
            edges.append(copy_to(np_ref, n6_ref.at[back], ssem.at[2 + back], rsem.at[2 + back], where[k]))
    for c in edges:
        c.start()
    total = g_ref[la].astype(F32)
    for k in range(1, nla):
        copy_to(g_ref.at[la], buf1.at[k], s1.at[nla - k], r1.at[k], (la, lo)).wait_recv()
        total = total + buf1[k].astype(F32)
    mid[...] = total

    second = []
    for k in range(1, nlo):
        to = lon_at(k)
        c = copy_to(mid.at[pl.ds(jnp.minimum(to * pp, parts - pp), pp)], buf2.at[nlo - k], s2.at[k], r2.at[nlo - k], (la, to))
        c.start()
        second.append(c)
    piece = mid[pl.ds(jnp.minimum(lo * pp, parts - pp), pp)]
    for k in range(1, nlo):
        copy_to(mid.at[0:pp], buf2.at[k], s2.at[k], r2.at[k], (la, lo)).wait_recv()
        piece = piece + buf2[k]
    own[...] = piece.astype(BF16)

    third = []
    for k in range(1, nlo):
        c = copy_to(own, fin.at[pl.ds(lo * pp, pp)], s3.at[k], r3.at[nlo - k], (la, lon_at(k)))
        c.start()
        third.append(c)
    fin[pl.ds(lo * pp, pp)] = own[...]
    for k in range(1, nlo):
        copy_to(own, fin.at[pl.ds(lon_at(k) * pp, pp)], s3.at[k], r3.at[k], (la, lo)).wait_recv()

    fourth = []
    for k in range(1, nla):
        c = copy_to(fin.at[0:parts], gs_ref.at[la], s4.at[k], r4.at[nla - k], (lat_at(k), lo))
        c.start()
        fourth.append(c)
    gs_ref[la] = fin[0:parts]
    for k in range(1, nla):
        copy_to(fin.at[0:parts], gs_ref.at[lat_at(k)], s4.at[k], r4.at[k], (la, lo)).wait_recv()
    for c in edges:
        c.wait_recv()
    for c in edges + first + second + third + fourth:
        c.wait_send()


def finish_kernel(num_ref, inv_ref, nu_ref, nd_ref, n6_ref, g_ref, b_ref, gi_ref, gm_ref, go_ref, scr):
    la, nla = lax.axis_index("lat"), lax.axis_size("lat")
    keep_top = jnp.where(la > 0, 1.0, 0.0).astype(F32)
    keep_bot = jnp.where(la < nla - 1, 1.0, 0.0).astype(F32)
    lane = lanes_of((CH, 128))

    def left_of(k, t):
        v = pltpu.roll(n6_ref[k - 2].astype(F32), (128 - MG * t) % 128, 1) if t else n6_ref[k - 2].astype(F32)
        return jnp.where(lane < MG, v, 0.0)

    def right_of(k, t):
        v = pltpu.roll(n6_ref[k - 2].astype(F32), (64 - MG - MG * t) % 128, 1)
        return jnp.where(lane >= 128 - MG, v, 0.0)

    for r in range(TR):
        v = num_ref[r]
        if r < MG:
            v = v + keep_top * nu_ref[r].astype(F32)
            hl = left_of(LF, r + MG) + keep_top * left_of(UL, r + MG + TR)
            hr = right_of(RT, r + MG) + keep_top * right_of(UR, r + MG + TR)
        else:
            v = v + keep_bot * nd_ref[r - MG].astype(F32)
            hl = left_of(LF, r + MG) + keep_bot * left_of(DL, r - MG)
            hr = right_of(RT, r + MG) + keep_bot * right_of(DR, r - MG)
        v = v + jnp.concatenate([hl, hr], axis=1)
        v = v * inv_ref[r : r + 1, :]
        for half in range(2):
            scr[half, pl.ds(r, CH, stride=TR), :] = v[:, half * 128 : half * 128 + 128]
    for half in range(2):
        b_ref[:, half * 128 : half * 128 + 128] = scr[half]
    for tap in range(9):
        gm_ref[tap] = g_ref[G_MID + tap * WD : G_MID + (tap + 1) * WD].astype(F32)
        go_ref[tap] = g_ref[G_OUT + tap * CH : G_OUT + (tap + 1) * CH].astype(F32)
        gi_ref[tap] = g_ref[G_IN + tap * CH : G_IN + (tap + 1) * CH].astype(F32).T


def sds(shape, dtype):
    return jax.ShapeDtypeStruct(shape, dtype)


def shards(sizes, fields, cotangent, kernel_in, kernel_mid, kernel_out, patch_anchors, blend_weights, tile_counts):
    nla, nlo = sizes
    anch = patch_anchors[0, 0]
    dma = pltpu.SemaphoreType.DMA
    fc, edge, canv = pl.pallas_call(
        prep_kernel,
        name="prepare",
        out_shape=(sds((TR, 2 * CH, TC), BF16), sds((2 * CH, 128), BF16), sds((2 * TR, EXT), BF16)),
        in_specs=smem(2) + vmem(3),
        out_specs=vmem(3),
        scratch_shapes=[pltpu.VMEM((4, CH * TR, 128), F32)],
    )(anch, tile_counts, fields, cotangent, blend_weights)

    up, dn, en, cn = pl.pallas_call(
        functools.partial(exchange_kernel, sizes),
        name="exchange",
        out_shape=(
            sds((MG, 2 * CH, TC), BF16), sds((MG, 2 * CH, TC), BF16),
            sds((6, 2 * CH, 128), BF16), sds((8, 2 * TR, EXT), BF16),
        ),
        in_specs=vmem(3),
        out_specs=vmem(4),
        scratch_shapes=[dma((16,)), dma((16,))],
        compiler_params=pltpu.CompilerParams(collective_id=0, has_side_effects=True),
    )(fc, edge, canv)

    win = kernel_in.transpose(1, 0, 2).reshape(WD, 9 * CH)
    wmid = kernel_mid.transpose(1, 0, 2).reshape(WD, 9 * WD)
    wout = kernel_out.reshape(9 * CH, WD)
    woutt = kernel_out[::-1].transpose(2, 0, 1).reshape(WD, 9 * CH)
    wmidt = kernel_mid[::-1].transpose(2, 0, 1).reshape(WD, 9 * WD)

    parts = -(-(G_END // 8) // nla)
    pp = -(-parts // nlo)
    grow = nla * parts * 8
    vm = pltpu.VMEM
    num, top, bot, npk, grads, inv = pl.pallas_call(
        patch_kernel,
        name="patches",
        out_shape=(
            sds((TR, CH, TC), F32), sds((MG, CH, TC), BF16), sds((MG, CH, TC), BF16),
            sds((CH, 128), BF16), sds((grow, WD), BF16), sds((TR, TC), F32),
        ),
        in_specs=smem(2) + vmem(12),
        out_specs=vmem(6),
        scratch_shapes=[
            vm((2 * TR, 2 * CH, EXT), BF16), vm((2 * TR, EXT), F32),
            vm((3 * CH, PAD), BF16), vm((3 * CH, PAD), BF16), vm((3 * WD, PAD), BF16), vm((3 * WD, PAD), BF16),
            vm((WD, CELLS), BF16), vm((WD, CELLS), BF16), vm((WD, CELLS), F32), vm((8, 128), F32),
            vm((WD, CELLS), F32), vm((WD, CELLS), BF16), vm((TR + 2, 3 * CH, TC), F32),
            vm((2 * TR, CH, EXT), F32), vm((WD, 9 * WD), F32), vm((3, 3 * CH, WD), F32), vm((3, 3 * CH, WD), F32),
        ],
    )(anch, tile_counts, fc, up, dn, en, canv, cn, blend_weights, win, wmid, wout, woutt, wmidt)

    nu, nd, n6, gs = pl.pallas_call(
        functools.partial(reduce_kernel, sizes, parts),
        name="reduce",
        out_shape=(
            sds((MG, CH, TC), BF16), sds((MG, CH, TC), BF16), sds((6, CH, 128), BF16),
            sds((nla, parts, 8, WD), BF16),
        ),
        in_specs=vmem(4),
        out_specs=vmem(4),
        scratch_shapes=[
            vm((nla, parts, 8, WD), BF16), vm((nlo, pp, 8, WD), F32), vm((parts, 8, WD), F32),
            vm((pp, 8, WD), BF16), vm((nlo * pp, 8, WD), BF16),
            dma((8,)), dma((8,)), dma((nla,)), dma((nla,)), dma((nlo,)), dma((nlo,)),
            dma((nlo,)), dma((nlo,)), dma((nla,)), dma((nla,)),
        ],
        compiler_params=pltpu.CompilerParams(collective_id=1, has_side_effects=True),
    )(top, bot, npk, grads.reshape(nla, parts, 8, WD))

    blended, gi, gm, go = pl.pallas_call(
        finish_kernel,
        name="finish",
        out_shape=(
            sds((CH * TR, TC), F32), sds((9, WD, CH), F32), sds((9, WD, WD), F32), sds((9, CH, WD), F32),
        ),
        in_specs=vmem(6),
        out_specs=vmem(4),
        scratch_shapes=[vm((2, CH * TR, 128), F32)],
    )(num, inv, nu, nd, n6, gs.reshape(grow, WD))
    return blended.reshape(CH, TR, TC), gi, gm, go


def solution(mesh):
    sizes = (mesh.shape["lat"], mesh.shape["lon"])
    return jax.shard_map(
        functools.partial(shards, sizes),
        mesh=mesh,
        in_specs=(
            P(None, "lat", "lon"), P(None, "lat", "lon"), P(), P(), P(),
            P("lat", "lon", None, None), P(None, "lat", "lon"), P("lat", "lon"),
        ),
        out_specs=(P(None, "lat", "lon"), P(), P(), P()),
        check_vma=False,
    )
```

time: 508 us -> 126 us (0.25); the launches traced: 499 us -> 125 us
  waiting for transfers between devices: 275 us -> 0 us
  Pallas kernels: 0 us -> 116 us
  matrix products: 60.3 us -> 0 us
  starting transfers between devices: 58.3 us -> 0 us
  local copies, waits for them, and re-layouts: 62.7 us -> 7.72 us
  between operations: 30.9 us -> 1.31 us
  other arithmetic: 10.7 us -> 0 us
    psum x1 -> x0, waiting for transfers between devices: 249 us -> none  [shards(): summed_grads = lax.psum((totals[0], totals[1], totals[2]), ('lat', 'lon'))]
    pallas_call x0 -> x5, Pallas kernels: none -> 116 us  [the longest x1 63.5 us: shards(): pl.pallas_call(patch_kernel, name='patches', out_shape=(sds((TR, CH, TC),...]
    dot_general x144 -> x0, matrix products: 60.3 us -> none  [the longest x54 25.4 us: kernel_grad(): jnp.einsum('ohw,khw->ok', cotangent, padded[:, tap_row:tap_row + height,...]
    ppermute x19 -> x0, starting transfers between devices: 58.3 us -> none  [the longest x8 44.2 us: extended_2(): lax.ppermute(lax.slice_in_dim(block, 0, width, axis=dim), axis, backward)]
    dynamic_update_slice x10 -> x0, local copies, waits for them, and re-layouts: 44 us -> none  [the longest x8 43.7 us: place_slots(): lax.dynamic_update_slice(canvas, current + per_slot[slot_index], corner)]
    ppermute x19 -> x0, waiting for transfers between devices: 26.1 us -> none  [the longest x3 13 us: shifted(): return lax.ppermute(value, axis, pairs)]
    while x20 -> x0, local copies, waits for them, and re-layouts: 5.21 us -> none
  transfers between devices with their start and end apart: 20 -> 0, of which waited for: 9 -> 0; matrix products, arithmetic and copies ran while one was open for 1% -> 0% of each run, Pallas kernels for 0% -> 0%
where the time goes in v1:
time: 126 us; the launch traced here: 125 us
  Pallas kernels  116 us (92%)
  local copies, waits for them, and re-layouts  7.72 us (6%)
  between operations  1.31 us (1%)
    pallas_call x1, Pallas kernels, shards(): pl.pallas_call(patch_kernel, name='patches', out_shape=(sds((TR, CH, TC),...  63.5 us
    pallas_call x1, Pallas kernels, shards(): pl.pallas_call(functools.partial(reduce_kernel, sizes, parts), name='redu...  31 us
    pallas_call x1, Pallas kernels, shards(): pl.pallas_call(functools.partial(exchange_kernel, sizes), name='exchange'...  17.6 us
    unnamed x8, local copies, waits for them, and re-layouts  2.83 us
    pallas_call x1, Pallas kernels, shards(): pl.pallas_call(finish_kernel, name='finish', out_shape=(sds((CH * TR, TC)...  2.53 us

profile of v1, /device:TPU:1, one launch (start us, length us, event | category | flops | bytes accessed | tf_op | source)
XLA Modules:
  0.0 125.4 jit_solution(11409247927122187856)
XLA Ops:
  1.3 0.0 copy-start.2
  1.3 0.7 copy-done.2
  2.0 0.7 copy.21.anch
  2.6 0.0 copy-start.1
  2.6 0.9 rev.6
  3.5 0.0 copy-start
  3.5 0.8 copy.24.woutt_ref
  4.3 0.0 copy-done.1
  4.3 0.8 copy.22.win_ref
  5.1 1.8 %prepare.1 = (bf16[8,64,256]{2,1,0:T(8,128)(2,1)}, bf16[64,128]{1,0:T(8,128)(2,1)}, bf16[16,384]{1,0:T(8,128)(2,1)}) custom-call(s32[4,2]{1,0:T(4,128)} %copy.21.anch, s32[1,1]{1,0:T(1,128)S(6)} %copy.27.cnt, bf16[32,8,256]{2,1,0:T(8,128)(2,1)} %f_ref.1, bf16[32,8,256]{2,1,0:T(8,128)(2,1)} %c_ref.1, s32[4,8,256]{2,1,0:T(8,128)} %w_ref.3), custom_call_target="tpu_custom_call" | custom-call | tf_op jit(solution)/shard_map/prepare/pallas_call | solution.py:417
  6.9 0.0 copy-done
  6.9 0.9 copy.25.wmidt_ref
  7.8 0.2 copy.20
  8.0 0.9 copy.23.wmid_ref
  8.9 17.6 %exchange.1 = (bf16[4,64,256]{2,1,0:T(8,128)(2,1)}, bf16[4,64,256]{2,1,0:T(8,128)(2,1)}, bf16[6,64,128]{2,1,0:T(8,128)(2,1)}, bf16[8,16,384]{2,1,0:T(8,128)(2,1)}) custom-call(bf16[8,64,256]{2,1,0:T(8,128)(2,1)} %get-tuple-element.25.fc_ref, bf16[64,128]{1,0:T(8,128)(2,1)} %get-tuple-element.26.e_ref, bf16[16,384]{1,0:T(8,128)(2,1)} %get-tuple-element.27.cv_ref), custom_call_target="tpu_custom_call" | custom-call | tf_op jit(solution)/shard_map/exchange/pallas_call | solution.py:426
  26.5 63.5 %patches.1 = (f32[8,32,256]{2,1,0:T(8,128)}, bf16[4,32,256]{2,1,0:T(8,128)(2,1)}, bf16[4,32,256]{2,1,0:T(8,128)(2,1)}, bf16[32,128]{1,0:T(8,128)(2,1)}, bf16[1792,128]{1,0:T(8,128)(2,1)}, /*index=5*/f32[8,256]{1,0:T(8,128)}) custom-call(s32[4,2]{1,0:T(4,128)} %copy.21.anch, s32[1,1]{1,0:T(1,128)S(6)} %copy.27.cnt, ...), custom_call_target="tpu_custom_call" | custom-call | tf_op jit(solution)/shard_map/patches/pallas_call | solution.py:449
  89.9 31.0 %reduce.1 = (bf16[4,32,256]{2,1,0:T(8,128)(2,1)}, bf16[4,32,256]{2,1,0:T(8,128)(2,1)}, bf16[6,32,128]{2,1,0:T(8,128)(2,1)}, bf16[16,14,8,128]{3,2,1,0:T(8,128)(2,1)}) custom-call(bf16[4,32,256]{2,1,0:T(8,128)(2,1)} %get-tuple-element.34.top_ref, bf16[4,32,256]{2,1,0:T(8,128)(2,1)} %get-tuple-element.35.bot_ref, bf16[32,128]{1,0:T(8,128)(2,1)} %get-tuple-element.36.np_ref, ...), custom_call_target="tpu_custom_call" | custom-call | tf_op jit(solution)/shard_map/reduce/pallas_call | solution.py:467
  120.9 2.5 %finish.1 = (f32[256,256]{1,0:T(8,128)}, f32[9,128,32]{2,1,0:T(8,128)}, f32[9,128,128]{2,1,0:T(8,128)}, f32[9,32,128]{2,1,0:T(8,128)}) custom-call(f32[8,32,256]{2,1,0:T(8,128)} %get-tuple-element.32.num_ref, f32[8,256]{1,0:T(8,128)} %get-tuple-element.33.inv_ref, bf16[4,32,256]{2,1,0:T(8,128)(2,1)} %get-tuple-element.38.nu_ref, ...), custom_call_target="tpu_custom_call" | custom-call | tf_op jit(solution)/shard_map/finish/pallas_call | solution.py:485
  123.5 1.9 %copy.26 = f32[9,128,32]{1,2,0:T(8,128)} copy(f32[9,128,32]{2,1,0:T(8,128)} %get-tuple-element.51) | data formatting | bytes 294912
  (1 shorter events, 0.0 us)
Async XLA Ops:
  1.3 0.7 copy-start.2
  2.6 1.7 %copy-start.1 = (bf16[9,128,32]{1,2,0:T(8,128)(2,1)S(1)}, bf16[9,128,32]{1,2,0:T(8,128)(2,1)}, u32[]{:S(2)}) copy-start(bf16[9,128,32]{1,2,0:T(8,128)(2,1)} %param.10) | copy-start | bytes 221188
  3.5 3.3 %copy-start = (bf16[9,128,128]{2,1,0:T(8,128)(2,1)S(1)}, bf16[9,128,128]{2,1,0:T(8,128)(2,1)}, u32[]{:S(2)}) copy-start(bf16[9,128,128]{2,1,0:T(8,128)(2,1)} %param.11) | copy-start | bytes 884740

commit v2 on v1

--- a/solution.py
+++ b/solution.py
@@ -99,23 +99,25 @@
 
 
 def shift_cols(x, step):
-    lane = lanes_of(x.shape)
+    lane = lanes_of((x.shape[0], 128))
+    lo, hi = x[:, :128], x[:, 128:]
+    zero = jnp.zeros_like(lo)
     if step < 0:
-        return jnp.where(lane == 0, 0.0, pltpu.roll(x, 1, 1))
-    return jnp.where(lane == x.shape[1] - 1, 0.0, pltpu.roll(x, x.shape[1] - 1, 1))
+        lo, hi = pltpu.roll(lo, 1, 1), pltpu.roll(hi, 1, 1)
+        return jnp.concatenate([jnp.where(lane == 0, zero, lo), jnp.where(lane == 0, lo, hi)], axis=1)
+    lo, hi = pltpu.roll(lo, 127, 1), pltpu.roll(hi, 127, 1)
+    return jnp.concatenate([jnp.where(lane == 127, hi, lo), jnp.where(lane == 127, zero, hi)], axis=1)
 
 
 def put_shifted(buf, r, x, ch):
-    at = pl.multiple_of((r + 1) * TC, TC)
-    buf[0:ch, pl.ds(at, TC)] = shift_cols(x, -1).astype(BF16)
-    buf[ch : 2 * ch, pl.ds(at, TC)] = x.astype(BF16)
-    buf[2 * ch : 3 * ch, pl.ds(at, TC)] = shift_cols(x, 1).astype(BF16)
-
-
-def stacked(buf, r):
-    return jnp.concatenate(
-        [buf[:, pl.ds(pl.multiple_of((r + dy) * TC, TC), TC)] for dy in range(3)], axis=0
-    )
+    at = slice((r + 1) * TC, (r + 2) * TC)
+    buf[0:ch, at] = shift_cols(x, -1)
+    buf[ch : 2 * ch, at] = x
+    buf[2 * ch : 3 * ch, at] = shift_cols(x, 1)
+
+
+def four_rows(buf, i, rows=slice(None)):
+    return jnp.concatenate([buf[rows, (2 * i + j) * TC : (2 * i + j + 1) * TC] for j in range(4)], axis=0)
 
 
 def dot(a, b):
@@ -129,7 +131,7 @@
 def patch_kernel(
     anch, cnt, fc_ref, up_ref, dn_ref, en_ref, cv_ref, cn_ref, w_ref, win_ref, wmid_ref, wout_ref,
     woutt_ref, wmidt_ref, num_ref, top_ref, bot_ref, np_ref, g_ref, inv_ref,
-    ext, inv, xpb, dpb, h1b, dzb, h1, h2, sl1, sl2, dh2, dz1, oq, canvas, gmid, gout, gin,
+    ext, inv, xpb, dpb, h1b, dzb, h2b, sl1, dh2, dz1, canvas, gmid, gout, gin,
 ):
     la, nla = lax.axis_index("lat"), lax.axis_size("lat")
     keep_top = la > 0
@@ -178,7 +180,7 @@
         ext[t, 0:CH, :] = row[:CH].astype(BF16)
         ext[t, CH:, :] = (row[CH:] * inv[t : t + 1, :]).astype(BF16)
 
-    for buf in (xpb, dpb, h1b, dzb):
+    for buf in (xpb, dpb, h1b, dzb, h2b):
         z = jnp.zeros((buf.shape[0], TC), BF16)
         buf[:, 0:TC] = z
         buf[:, PAD - TC : PAD] = z
@@ -190,76 +192,90 @@
     def one_patch(q, carry):
         a, b = anch[q, 0], anch[q, 1]
         turn = lax.rem(EXT + MG - b, EXT)
-
-        def window(r, c):
-            x = pltpu.roll(ext[a + r].astype(F32), turn, 1)[:, :TC]
-            pw = w_ref[q, pl.ds(r, 1), :].astype(F32)
-            put_shifted(xpb, r, x[:CH], CH)
-            put_shifted(dpb, r, x[CH:] * pw, CH)
-            return c
-
-        lax.fori_loop(0, TR, window, 0)
-
-        def first(r, c):
-            at = pl.ds(pl.multiple_of(r * TC, TC), TC)
-            z = dot(win_ref[...], stacked(xpb, r))
-            s = 0.5 + 0.5 * jnp.tanh(0.5 * z)
-            h = z * s
-            h1[:, at] = h.astype(BF16)
-            put_shifted(h1b, r, h, WD)
-            sl1[:, at] = s * (1.0 + z * (1.0 - s))
-            return c
-
-        lax.fori_loop(0, TR, first, 0)
-
-        oq[...] = jnp.zeros_like(oq)
-
-        def second(r, c):
-            at = pl.ds(pl.multiple_of(r * TC, TC), TC)
-            z = dot(wmid_ref[...], stacked(h1b, r))
-            s = 0.5 + 0.5 * jnp.tanh(0.5 * z)
-            h = (h1[:, at].astype(F32) + z * s).astype(BF16)
-            h2[:, at] = h
-            slope = s * (1.0 + z * (1.0 - s))
-            p = dot(wout_ref[...], h)
-            for dy in range(3):
-                oq[r + 2 - dy] += p[dy * 96 : (dy + 1) * 96]
-            g = dot(woutt_ref[...], stacked(dpb, r))
-            dh2[:, at] = g
-            put_shifted(dzb, r, g * slope, WD)
-            return c
-
-        lax.fori_loop(0, TR, second, 0)
-
         place = lax.rem(b + (EXT - MG), EXT)
-
-        def blend(r, c):
-            v = oq[r + 1]
-            o = shift_cols(v[0:CH], -1) + v[CH : 2 * CH] + shift_cols(v[2 * CH :], 1)
-            o = o * w_ref[q, pl.ds(r, 1), :].astype(F32)
-            o = jnp.concatenate([o, jnp.zeros((CH, 128), F32)], axis=1)
-            canvas[a + r] += pltpu.roll(o, place, 1)
-            return c
-
-        lax.fori_loop(0, TR, blend, 0)
-
-        def third(r, c):
-            at = pl.ds(pl.multiple_of(r * TC, TC), TC)
-            g = dh2[:, at] + dot(wmidt_ref[...], stacked(dzb, r))
-            dz1[:, at] = (g * sl1[:, at]).astype(BF16)
-            return c
-
-        lax.fori_loop(0, TR, third, 0)
-
-        hh = h2[...]
+        weights = w_ref[q].astype(F32)
+
+        def rows(i):
+            return range(2 * i, 2 * i + 2)
+
+        def at(r):
+            return slice(r * TC, (r + 1) * TC)
+
+        def half(z, r):
+            n = z.shape[0] // 2
+            return z[:n] if r % 2 == 0 else z[n:]
+
+        def window(i):
+            for r in rows(i):
+                x = pltpu.roll(ext[a + r].astype(F32), turn, 1)[:, :TC]
+                put_shifted(xpb, r, x[:CH].astype(BF16), CH)
+                put_shifted(dpb, r, (x[CH:] * weights[r : r + 1, :]).astype(BF16), CH)
+
+        def first(i):
+            zz = dot(win_ref[...], four_rows(xpb, i))
+            for r in rows(i):
+                z = half(zz, r)
+                t = jnp.tanh(0.5 * z)
+                s = 0.5 + 0.5 * t
+                h = z * s
+                put_shifted(h1b, r, h.astype(BF16), WD)
+                sl1[:, at(r)] = s + h * (1.0 - s)
+
+        def second(i):
+            zz = dot(wmid_ref[...], four_rows(h1b, i))
+            gg = dot(woutt_ref[...], four_rows(dpb, i))
+            for r in rows(i):
+                z, g = half(zz, r), half(gg, r)
+                t = jnp.tanh(0.5 * z)
+                s = 0.5 + 0.5 * t
+                h = z * s
+                h2b[:, at(r + 1)] = (h1b[WD : 2 * WD, at(r + 1)].astype(F32) + h).astype(BF16)
+                dh2[:, at(r)] = g
+                put_shifted(dzb, r, (g * (s + h * (1.0 - s))).astype(BF16), WD)
+
+        def blend(i):
+            oo = dot(wout_ref[...], four_rows(h2b, i))
+            for r in rows(i):
+                v = half(oo, r)
+                o = shift_cols(v[0:CH], -1) + v[CH : 2 * CH] + shift_cols(v[2 * CH :], 1)
+                o = o * weights[r : r + 1, :]
+                o = jnp.concatenate([o, jnp.zeros((CH, 128), F32)], axis=1)
+                canvas[a + r] += pltpu.roll(o, place, 1)
+
+        def third(i):
+            zz = dot(wmidt_ref[...], four_rows(dzb, i))
+            for r in rows(i):
+                g = dh2[:, at(r)] + half(zz, r)
+                dz1[:, at(r)] = (g * sl1[:, at(r)]).astype(BF16)
+
+        window(0)
+        window(1)
+        first(0)
+        window(2)
+        first(1)
+        window(3)
+        second(0)
+        first(2)
+        second(1)
+        first(3)
+        third(0)
+        blend(0)
+        second(2)
+        third(1)
+        blend(1)
+        second(3)
+        third(2)
+        blend(2)
+        third(3)
+        blend(3)
+
+        hh = h2b[:, TC : TC + CELLS]
+        d1 = dz1[...]
+        d2 = dzb[0 : 2 * WD, TC : TC + CELLS]
         for dy in range(3):
+            gmid[dy] += dot_t(d2, h1b[0 : 2 * WD, dy * TC : dy * TC + CELLS])
             gout[dy] += dot_t(dpb[:, (2 - dy) * TC : (2 - dy) * TC + CELLS], hh)
-        d1 = dz1[...]
-        for dy in range(3):
             gin[dy] += dot_t(xpb[:, dy * TC : dy * TC + CELLS], d1)
-        d2 = dzb[WD : 2 * WD, TC : TC + CELLS]
-        for dy in range(3):
-            gmid[:, dy * 384 : (dy + 1) * 384] += dot_t(d2, h1b[:, dy * TC : dy * TC + CELLS])
         return carry
 
     lax.fori_loop(0, cnt[0, 0], one_patch, 0)
@@ -280,8 +296,11 @@
         pk = jnp.where((pk_lane >= at) & (pk_lane < at + MG), lo, pk)
     np_ref[...] = pk.astype(BF16)
     for tap in range(9):
-        g_ref[G_MID + tap * WD : G_MID + (tap + 1) * WD] = gmid[:, tap * WD : (tap + 1) * WD].astype(BF16)
         dy, dx = divmod(tap, 3)
+        ro, co = ((1, 0), (1, 1), (0, 1))[dx]
+        g_ref[G_MID + tap * WD : G_MID + (tap + 1) * WD] = gmid[
+            dy, ro * WD : (ro + 1) * WD, co * WD : (co + 1) * WD
+        ].astype(BF16)
         s = 2 - dx
         g_ref[G_OUT + tap * CH : G_OUT + (tap + 1) * CH] = gout[dy, s * CH : (s + 1) * CH].astype(BF16)
         g_ref[G_IN + tap * CH : G_IN + (tap + 1) * CH] = gin[dy, dx * CH : (dx + 1) * CH].astype(BF16)
@@ -436,11 +455,15 @@
         compiler_params=pltpu.CompilerParams(collective_id=0, has_side_effects=True),
     )(fc, edge, canv)
 
-    win = kernel_in.transpose(1, 0, 2).reshape(WD, 9 * CH)
-    wmid = kernel_mid.transpose(1, 0, 2).reshape(WD, 9 * WD)
-    wout = kernel_out.reshape(9 * CH, WD)
-    woutt = kernel_out[::-1].transpose(2, 0, 1).reshape(WD, 9 * CH)
-    wmidt = kernel_mid[::-1].transpose(2, 0, 1).reshape(WD, 9 * WD)
+    def two_rows(w):
+        k = w.shape[1] // 3
+        return jnp.concatenate([jnp.pad(w, ((0, 0), (0, k))), jnp.pad(w, ((0, 0), (k, 0)))], axis=0)
+
+    win = two_rows(kernel_in.transpose(1, 0, 2).reshape(WD, 9 * CH))
+    wmid = two_rows(kernel_mid.transpose(1, 0, 2).reshape(WD, 9 * WD))
+    wout = two_rows(kernel_out.reshape(3, 3, CH, WD).transpose(1, 2, 0, 3).reshape(3 * CH, 3 * WD))
+    woutt = two_rows(kernel_out[::-1].transpose(2, 0, 1).reshape(WD, 9 * CH))
+    wmidt = two_rows(kernel_mid[::-1].transpose(2, 0, 1).reshape(WD, 9 * WD))
 
     parts = -(-(G_END // 8) // nla)
     pp = -(-parts // nlo)
@@ -458,9 +481,8 @@
         scratch_shapes=[
             vm((2 * TR, 2 * CH, EXT), BF16), vm((2 * TR, EXT), F32),
             vm((3 * CH, PAD), BF16), vm((3 * CH, PAD), BF16), vm((3 * WD, PAD), BF16), vm((3 * WD, PAD), BF16),
-            vm((WD, CELLS), BF16), vm((WD, CELLS), BF16), vm((WD, CELLS), F32), vm((8, 128), F32),
-            vm((WD, CELLS), F32), vm((WD, CELLS), BF16), vm((TR + 2, 3 * CH, TC), F32),
-            vm((2 * TR, CH, EXT), F32), vm((WD, 9 * WD), F32), vm((3, 3 * CH, WD), F32), vm((3, 3 * CH, WD), F32),
+            vm((WD, PAD), BF16), vm((WD, CELLS), F32), vm((WD, CELLS), F32), vm((WD, CELLS), BF16),
+            vm((2 * TR, CH, EXT), F32), vm((3, 2 * WD, 2 * WD), F32), vm((3, 3 * CH, WD), F32), vm((3, 3 * CH, WD), F32),
         ],
     )(anch, tile_counts, fc, up, dn, en, canv, cn, blend_weights, win, wmid, wout, woutt, wmidt)
 

time: 126 us -> 86.3 us (0.68)
  Pallas kernels: 116 us -> 75 us
  other arithmetic: 0 us -> 2.85 us
    pallas_call x1, Pallas kernels: 63.5 us -> 21.9 us  [shards(): pl.pallas_call(patch_kernel, name='patches', out_shape=(sds((TR, CH, TC),...]
    concatenate x0 -> x3, other arithmetic: none -> 2.85 us  [two_rows(): jnp.concatenate([jnp.pad(w, ((0, 0), (0, k))), jnp.pad(w, ((0, 0), (k, 0)...]
    reshape x4 -> x5, local copies, waits for them, and re-layouts: 3.29 us -> 2.53 us  [the longest x1 1 us: shards(): win = two_rows(kernel_in.transpose(1, 0, 2).reshape(WD, 9 * CH))]
    unnamed x8 -> x5, local copies, waits for them, and re-layouts: 2.83 us -> 2.17 us
where the time goes in v2:
time: 86.3 us; the launch traced here: 86.1 us
  Pallas kernels  75 us (87%)
  local copies, waits for them, and re-layouts  6.96 us (8%)
  other arithmetic  2.85 us (3%)
  between operations  1.33 us (2%)
    pallas_call x1, Pallas kernels, shards(): pl.pallas_call(functools.partial(reduce_kernel, sizes, parts), name='redu...  31 us
    pallas_call x1, Pallas kernels, shards(): pl.pallas_call(patch_kernel, name='patches', out_shape=(sds((TR, CH, TC),...  21.9 us
    pallas_call x1, Pallas kernels, shards(): pl.pallas_call(functools.partial(exchange_kernel, sizes), name='exchange'...  17.7 us
    concatenate x3, other arithmetic, two_rows(): jnp.concatenate([jnp.pad(w, ((0, 0), (0, k))), jnp.pad(w, ((0, 0), (k, 0)...  2.85 us
    pallas_call x1, Pallas kernels, shards(): pl.pallas_call(finish_kernel, name='finish', out_shape=(sds((CH * TR, TC)...  2.53 us
    unnamed x5, local copies, waits for them, and re-layouts  2.17 us
    pallas_call x1, Pallas kernels, shards(): pl.pallas_call(prep_kernel, name='prepare', out_shape=(sds((TR, 2 * CH, T...  1.81 us

profile of v2, /device:TPU:1, one launch (start us, length us, event | category | flops | bytes accessed | tf_op | source)
XLA Modules:
  0.0 86.1 jit_solution(7587796722692780952)
XLA Ops:
  1.3 1.3 %copy.31.anch = s32[4,2]{1,0:T(4,128)} copy(s32[4,2]{0,1:T(2,128)} %bitcast.32) | data formatting | bytes 64 | tf_op jit(solution)/shard_map/squeeze | solution.py:434
  2.6 0.9 %rev.6 = bf16[9,32,128]{2,1,0:T(8,128)(2,1)S(1)} reverse(bf16[9,32,128]{2,1,0:T(8,128)(2,1)} %param.12), dimensions={0} | reverse | bytes 147456 | tf_op jit(solution)/shard_map/rev | solution.py:465
  3.5 0.1 copy.27
  3.6 1.0 %copy.21 = bf16[128,288]{1,0:T(8,128)(2,1)S(1)} copy(bf16[128,288]{0,1:T(8,128)(2,1)} %bitcast.31) | data formatting | bytes 147456 | tf_op jit(solution)/shard_map/reshape | solution.py:462
  4.7 0.0 copy-start
  4.7 1.0 %copy.26 = bf16[3,3,32,128]{3,0,2,1:T(4,128)(2,1)S(1)} copy(bf16[3,3,32,128]{3,2,1,0:T(8,128)(2,1)} %bitcast.28) | data formatting | bytes 147456 | tf_op jit(solution)/shard_map/reshape | solution.py:464
  5.7 0.7 fusion.12.wout_ref
  6.4 0.9 %fusion.13 = (bf16[256,384]{1,0:T(8,128)(2,1)}, bf16[256,384]{1,0:T(8,128)(2,1)}) fusion(bf16[128,288]{1,0:T(8,128)(2,1)S(1)} %copy.21, bf16[128,288]{1,0:T(8,128)(2,1)S(1)} %copy.27), kind=kLoop, calls=%fused_computation.19 | loop fusion | flops 1376256 | bytes 540672 | tf_op jit(solution)/shard_map/concatenate | solution.py:460
  7.2 1.8 %prepare.1 = (bf16[8,64,256]{2,1,0:T(8,128)(2,1)}, bf16[64,128]{1,0:T(8,128)(2,1)}, bf16[16,384]{1,0:T(8,128)(2,1)}) custom-call(s32[4,2]{1,0:T(4,128)} %copy.31.anch, s32[1,1]{1,0:T(1,128)S(6)} %copy.36.cnt, bf16[32,8,256]{2,1,0:T(8,128)(2,1)} %f_ref.1, bf16[32,8,256]{2,1,0:T(8,128)(2,1)} %c_ref.1, s32[4,8,256]{2,1,0:T(8,128)} %w_ref.3), custom_call_target="tpu_custom_call" | custom-call | tf_op jit(solution)/shard_map/prepare/pallas_call | solution.py:436
  9.1 0.0 copy-done
  9.1 0.2 copy.29
  9.3 0.2 copy.23
  9.5 0.2 copy.24
  9.7 17.7 %exchange.1 = (bf16[4,64,256]{2,1,0:T(8,128)(2,1)}, bf16[4,64,256]{2,1,0:T(8,128)(2,1)}, bf16[6,64,128]{2,1,0:T(8,128)(2,1)}, bf16[8,16,384]{2,1,0:T(8,128)(2,1)}) custom-call(bf16[8,64,256]{2,1,0:T(8,128)(2,1)} %get-tuple-element.25.fc_ref, bf16[64,128]{1,0:T(8,128)(2,1)} %get-tuple-element.26.e_ref, bf16[16,384]{1,0:T(8,128)(2,1)} %get-tuple-element.27.cv_ref), custom_call_target="tpu_custom_call" | custom-call | tf_op jit(solution)/shard_map/exchange/pallas_call | solution.py:445
  27.5 1.3 %fusion.4 = (bf16[256,1536]{1,0:T(8,128)(2,1)}, bf16[256,1536]{1,0:T(8,128)(2,1)}) fusion(bf16[128,1152]{1,0:T(8,128)(2,1)S(1)} %copy.24, bf16[128,1152]{1,0:T(8,128)(2,1)S(1)} %copy.29), kind=kLoop, calls=%fused_computation.6 | loop fusion | flops 5505024 | bytes 2162688 | tf_op jit(solution)/shard_map/concatenate | solution.py:460
  28.7 21.9 %patches.1 = (f32[8,32,256]{2,1,0:T(8,128)}, bf16[4,32,256]{2,1,0:T(8,128)(2,1)}, bf16[4,32,256]{2,1,0:T(8,128)(2,1)}, bf16[32,128]{1,0:T(8,128)(2,1)}, bf16[1792,128]{1,0:T(8,128)(2,1)}, /*index=5*/f32[8,256]{1,0:T(8,128)}) custom-call(s32[4,2]{1,0:T(4,128)} %copy.31.anch, s32[1,1]{1,0:T(1,128)S(6)} %copy.36.cnt, ...), custom_call_target="tpu_custom_call" | custom-call | tf_op jit(solution)/shard_map/patches/pallas_call | solution.py:472
  50.7 31.0 %reduce.1 = (bf16[4,32,256]{2,1,0:T(8,128)(2,1)}, bf16[4,32,256]{2,1,0:T(8,128)(2,1)}, bf16[6,32,128]{2,1,0:T(8,128)(2,1)}, bf16[16,14,8,128]{3,2,1,0:T(8,128)(2,1)}) custom-call(bf16[4,32,256]{2,1,0:T(8,128)(2,1)} %get-tuple-element.34.top_ref, bf16[4,32,256]{2,1,0:T(8,128)(2,1)} %get-tuple-element.35.bot_ref, bf16[32,128]{1,0:T(8,128)(2,1)} %get-tuple-element.36.np_ref, ...), custom_call_target="tpu_custom_call" | custom-call | tf_op jit(solution)/shard_map/reduce/pallas_call | solution.py:489
  81.7 2.5 %finish.1 = (f32[256,256]{1,0:T(8,128)}, f32[9,128,32]{2,1,0:T(8,128)}, f32[9,128,128]{2,1,0:T(8,128)}, f32[9,32,128]{2,1,0:T(8,128)}) custom-call(f32[8,32,256]{2,1,0:T(8,128)} %get-tuple-element.32.num_ref, f32[8,256]{1,0:T(8,128)} %get-tuple-element.33.inv_ref, bf16[4,32,256]{2,1,0:T(8,128)(2,1)} %get-tuple-element.38.nu_ref, ...), custom_call_target="tpu_custom_call" | custom-call | tf_op jit(solution)/shard_map/finish/pallas_call | solution.py:507
  84.2 1.9 %copy.32 = f32[9,128,32]{1,2,0:T(8,128)} copy(f32[9,128,32]{2,1,0:T(8,128)} %get-tuple-element.51) | data formatting | bytes 294912
  (2 shorter events, 0.0 us)
Async XLA Ops:
  4.7 4.4 %copy-start = (bf16[9,128,128]{2,1,0:T(8,128)(2,1)S(1)}, bf16[9,128,128]{2,1,0:T(8,128)(2,1)}, u32[]{:S(2)}) copy-start(bf16[9,128,128]{2,1,0:T(8,128)(2,1)} %param.11) | copy-start | bytes 884740

commit v3 on v2

--- a/solution.py
+++ b/solution.py
@@ -63,13 +63,47 @@
         live = jnp.where(q < cnt[0, 0], 1.0, 0.0).astype(F32)
         w = w_ref[q].astype(F32) * live
         w = jnp.concatenate([w, jnp.zeros((TR, 128), F32)], axis=1)
-        w = pltpu.roll(w, lax.rem(anch[q, 1] + (EXT - MG), EXT), 1)
+        w = pltpu.roll(w, lax.rem(anch[1, q] + (EXT - MG), EXT), 1)
         w = jnp.concatenate([w, jnp.zeros((TR, EXT), F32)], axis=0)
-        total = total + pltpu.roll(w, anch[q, 0], 0)
+        total = total + pltpu.roll(w, anch[0, q], 0)
     cv_ref[...] = total.astype(BF16)
 
 
-def exchange_kernel(sizes, fc_ref, e_ref, cv_ref, up_ref, dn_ref, en_ref, cn_ref, ssem, rsem):
+def two_rows(a):
+    k = a.shape[0] // 3
+    z = jnp.zeros((k, a.shape[1]), a.dtype)
+    return jnp.concatenate([a, z], axis=0), jnp.concatenate([z, a], axis=0)
+
+
+def lay_weights(ki_ref, km_ref, ko_ref, win_ref, wmid_ref, wout_ref, woutt_ref, wmidt_ref):
+    for dst, taps in (
+        (win_ref, [ki_ref[t] for t in range(9)]),
+        (woutt_ref, [ko_ref[8 - t] for t in range(9)]),
+    ):
+        one, two = two_rows(jnp.concatenate(taps, axis=0))
+        dst[0:WD] = one.T
+        dst[WD : 2 * WD] = two.T
+    zero = jnp.zeros((WD, 3 * WD), BF16)
+    for dst in (wmid_ref, wmidt_ref):
+        dst[0:WD, 9 * WD :] = zero
+        dst[WD : 2 * WD, : 3 * WD] = zero
+    for t in range(9):
+        for dst, w in ((wmid_ref, km_ref[t]), (wmidt_ref, km_ref[8 - t].T)):
+            dst[0:WD, t * WD : (t + 1) * WD] = w
+            dst[WD : 2 * WD, (t + 3) * WD : (t + 4) * WD] = w
+    zero = jnp.zeros((CH, WD), BF16)
+    for ro in range(2):
+        for dx in range(3):
+            for j in range(4):
+                w = ko_ref[3 * (j - ro) + dx] if 0 <= j - ro <= 2 else zero
+                at = (ro * 3 + dx) * CH
+                wout_ref[at : at + CH, j * WD : (j + 1) * WD] = w
+
+
+def exchange_kernel(
+    sizes, fc_ref, e_ref, cv_ref, ki_ref, km_ref, ko_ref, up_ref, dn_ref, en_ref, cn_ref,
+    win_ref, wmid_ref, wout_ref, woutt_ref, wmidt_ref, ssem, rsem,
+):
     la, lo = lax.axis_index("lat"), lax.axis_index("lon")
     nla, nlo = sizes
     where = [(lax.rem(la + di + nla, nla), lax.rem(lo + dj + nlo, nlo)) for di, dj in NB]
@@ -94,6 +128,7 @@
         send(cv_ref, cn_ref.at[back], where[k], 2 + back)
         if dj:
             send(e_ref, en_ref.at[back - 2], where[k], 10 + back - 2)
+    lay_weights(ki_ref, km_ref, ko_ref, win_ref, wmid_ref, wout_ref, woutt_ref, wmidt_ref)
     for copy in copies:
         copy.wait()
 
@@ -190,7 +225,7 @@
     gin[...] = jnp.zeros_like(gin)
 
     def one_patch(q, carry):
-        a, b = anch[q, 0], anch[q, 1]
+        a, b = anch[0, q], anch[1, q]
         turn = lax.rem(EXT + MG - b, EXT)
         place = lax.rem(b + (EXT - MG), EXT)
         weights = w_ref[q].astype(F32)
@@ -300,44 +335,58 @@
         ro, co = ((1, 0), (1, 1), (0, 1))[dx]
         g_ref[G_MID + tap * WD : G_MID + (tap + 1) * WD] = gmid[
             dy, ro * WD : (ro + 1) * WD, co * WD : (co + 1) * WD
-        ].astype(BF16)
+        ]
         s = 2 - dx
-        g_ref[G_OUT + tap * CH : G_OUT + (tap + 1) * CH] = gout[dy, s * CH : (s + 1) * CH].astype(BF16)
-        g_ref[G_IN + tap * CH : G_IN + (tap + 1) * CH] = gin[dy, dx * CH : (dx + 1) * CH].astype(BF16)
+        g_ref[G_OUT + tap * CH : G_OUT + (tap + 1) * CH] = gout[dy, s * CH : (s + 1) * CH]
+        g_ref[G_IN + tap * CH : G_IN + (tap + 1) * CH] = gin[dy, dx * CH : (dx + 1) * CH]
     if g_ref.shape[0] > G_END:
-        g_ref[G_END:] = jnp.zeros((g_ref.shape[0] - G_END, WD), BF16)
-
-
-def reduce_kernel(
-    sizes, parts, top_ref, bot_ref, np_ref, g_ref, nu_ref, nd_ref, n6_ref, gs_ref,
-    buf1, buf2, mid, own, fin, ssem, rsem, s1, r1, s2, r2, s3, r3, s4, r4,
-):
-    la, lo = lax.axis_index("lat"), lax.axis_index("lon")
+        g_ref[G_END:] = jnp.zeros((g_ref.shape[0] - G_END, WD), F32)
+
+
+class Place:
+    def __init__(self, dims):
+        self.dims = dims
+        yl, x, yh, z = dims
+        self.chips, self.depth = yh * yl * x, z
+        self.la, self.lo = lax.axis_index("lat"), lax.axis_index("lon")
+        self.core = lax.rem(self.la, 2)
+        self.z = lax.rem(self.lo, z)
+        self.chip = ((self.lo // z) * yl + self.la // (2 * x)) * x + lax.rem(self.la // 2, x)
+
+    def in_plane(self, k):
+        yl, x, yh, z = self.dims
+        chip = lax.rem(self.chip + k, self.chips)
+        y = chip // x
+        la = (lax.rem(y, yl) * x + lax.rem(chip, x)) * 2 + self.core
+        return chip, (la, (y // yl) * z + self.z)
+
+    def sibling(self):
+        return (self.la + 1 - 2 * self.core, self.lo)
+
+    def along_z(self, k):
+        z = lax.rem(self.z + k, self.depth)
+        return z, (self.la, self.lo - self.z + z)
+
+
+def copy_to(src, dst, ss, rs, dev):
+    return pltpu.make_async_remote_copy(
+        src_ref=src, dst_ref=dst, send_sem=ss, recv_sem=rs, device_id=dev, device_id_type=MESH
+    )
+
+
+def greet(place, sizes):
+    barrier = pltpu.get_barrier_semaphore()
     nla, nlo = sizes
-    pp = own.shape[0]
-    where = [(lax.rem(la + di + nla, nla), lax.rem(lo + dj + nlo, nlo)) for di, dj in NB]
-    lat_at = lambda k: lax.rem(la + k, nla)
-    lon_at = lambda k: lax.rem(lo + k, nlo)
-    barrier = pltpu.get_barrier_semaphore()
-    for dev in where:
+    where = [(lax.rem(place.la + di + nla, nla), lax.rem(place.lo + dj + nlo, nlo)) for di, dj in NB]
+    devs = where + [place.sibling()]
+    devs += [place.in_plane(k)[1] for k in range(1, place.chips)]
+    devs += [place.along_z(k)[1] for k in range(1, place.depth)]
+    for dev in devs:
         pl.semaphore_signal(barrier, inc=1, device_id=dev, device_id_type=MESH)
-    for k in range(1, nla):
-        pl.semaphore_signal(barrier, inc=1, device_id=(lat_at(k), lo), device_id_type=MESH)
-    for k in range(1, nlo):
-        pl.semaphore_signal(barrier, inc=1, device_id=(la, lon_at(k)), device_id_type=MESH)
-    pl.semaphore_wait(barrier, len(NB) + nla - 1 + nlo - 1)
-
-    def copy_to(src, dst, ss, rs, dev):
-        return pltpu.make_async_remote_copy(
-            src_ref=src, dst_ref=dst, send_sem=ss, recv_sem=rs, device_id=dev, device_id_type=MESH
-        )
-
-    first = []
-    for k in range(1, nla):
-        to = lat_at(k)
-        first.append(copy_to(g_ref.at[to], buf1.at[nla - k], s1.at[k], r1.at[nla - k], (to, lo)))
-    for c in first:
-        c.start()
+    return where, barrier, len(devs)
+
+
+def send_edges(where, top_ref, bot_ref, np_ref, nu_ref, nd_ref, n6_ref, ssem, rsem):
     edges = [
         copy_to(top_ref, nd_ref, ssem.at[0], rsem.at[0], where[UP]),
         copy_to(bot_ref, nu_ref, ssem.at[1], rsem.at[1], where[DN]),
@@ -348,44 +397,91 @@
             edges.append(copy_to(np_ref, n6_ref.at[back], ssem.at[2 + back], rsem.at[2 + back], where[k]))
     for c in edges:
         c.start()
-    total = g_ref[la].astype(F32)
-    for k in range(1, nla):
-        copy_to(g_ref.at[la], buf1.at[k], s1.at[nla - k], r1.at[k], (la, lo)).wait_recv()
-        total = total + buf1[k].astype(F32)
-    mid[...] = total
-
-    second = []
-    for k in range(1, nlo):
-        to = lon_at(k)
-        c = copy_to(mid.at[pl.ds(jnp.minimum(to * pp, parts - pp), pp)], buf2.at[nlo - k], s2.at[k], r2.at[nlo - k], (la, to))
+    return edges
+
+
+def sum_devices(place, g_ref, gs_ref, pair, rel, got, zs, zb, fin, sems):
+    n, depth, core = place.chips, place.depth, place.core
+    other = 1 - core
+    s0, r0, s1, r1, s2, r2, s3, r3, s4, r4 = sems
+    sib = place.sibling()
+    order = list(range(1, n)) + [0]
+
+    sent = []
+    for k in order:
+        chip, _ = place.in_plane(k)
+        c = copy_to(g_ref.at[other, chip], pair.at[k], s0.at[k], r0.at[k], sib)
         c.start()
-        second.append(c)
-    piece = mid[pl.ds(jnp.minimum(lo * pp, parts - pp), pp)]
-    for k in range(1, nlo):
-        copy_to(mid.at[0:pp], buf2.at[k], s2.at[k], r2.at[k], (la, lo)).wait_recv()
-        piece = piece + buf2[k]
-    own[...] = piece.astype(BF16)
-
-    third = []
-    for k in range(1, nlo):
-        c = copy_to(own, fin.at[pl.ds(lo * pp, pp)], s3.at[k], r3.at[nlo - k], (la, lon_at(k)))
+        sent.append(c)
+    mine = None
+    for k in order:
+        chip, dev = place.in_plane(k)
+        copy_to(g_ref.at[0, 0], pair.at[k], s0.at[k], r0.at[k], sib).wait_recv()
+        both = g_ref[core, chip] + pair[k]
+        if k:
+            rel[k] = both.astype(BF16)
+            c = copy_to(rel.at[k], got.at[n - k], s1.at[k], r1.at[n - k], dev)
+            c.start()
+            sent.append(c)
+        else:
+            mine = both
+    for k in range(1, n):
+        copy_to(rel.at[k], got.at[k], s1.at[k], r1.at[k], sib).wait_recv()
+        mine = mine + got[k].astype(F32)
+    zs[...] = mine.astype(BF16)
+    for k in range(1, depth):
+        _, dev = place.along_z(k)
+        c = copy_to(zs, zb.at[place.z], s2.at[k], r2.at[depth - k], dev)
         c.start()
-        third.append(c)
-    fin[pl.ds(lo * pp, pp)] = own[...]
-    for k in range(1, nlo):
-        copy_to(own, fin.at[pl.ds(lon_at(k) * pp, pp)], s3.at[k], r3.at[k], (la, lo)).wait_recv()
-
-    fourth = []
-    for k in range(1, nla):
-        c = copy_to(fin.at[0:parts], gs_ref.at[la], s4.at[k], r4.at[nla - k], (lat_at(k), lo))
+        sent.append(c)
+    zb[place.z] = zs[...]
+    for k in range(1, depth):
+        z, _ = place.along_z(k)
+        copy_to(zs, zb.at[z], s2.at[k], r2.at[k], sib).wait_recv()
+    total = zb[0].astype(F32)
+    for z in range(1, depth):
+        total = total + zb[z].astype(F32)
+    fin[...] = total.astype(BF16)
+    for k in range(1, n):
+        _, dev = place.in_plane(k)
+        c = copy_to(fin, gs_ref.at[core, place.chip], s3.at[k], r3.at[n - k], dev)
         c.start()
-        fourth.append(c)
-    gs_ref[la] = fin[0:parts]
-    for k in range(1, nla):
-        copy_to(fin.at[0:parts], gs_ref.at[lat_at(k)], s4.at[k], r4.at[k], (la, lo)).wait_recv()
+        sent.append(c)
+    c = copy_to(fin, gs_ref.at[core, place.chip], s4.at[0], r4.at[0], sib)
+    c.start()
+    sent.append(c)
+    gs_ref[core, place.chip] = fin[...]
+    for k in range(1, n):
+        chip, _ = place.in_plane(k)
+        copy_to(fin, gs_ref.at[core, chip], s3.at[k], r3.at[k], sib).wait_recv()
+        c = copy_to(gs_ref.at[core, chip], gs_ref.at[core, chip], s4.at[k], r4.at[k], sib)
+        c.start()
+        sent.append(c)
+    for k in range(n):
+        chip, _ = place.in_plane(k)
+        copy_to(fin, gs_ref.at[other, chip], s4.at[k], r4.at[k], sib).wait_recv()
+    return sent
+
+
+def sum_scratch(dims, rows):
+    yl, x, yh, z = dims
+    n = yl * x * yh
+    part = (rows, WD)
+    dma = pltpu.SemaphoreType.DMA
+    bufs = [pltpu.VMEM((n,) + part, F32)] + [pltpu.VMEM((n,) + part, BF16)] * 2
+    bufs += [pltpu.VMEM(part, BF16), pltpu.VMEM((z,) + part, BF16), pltpu.VMEM(part, BF16)]
+    return bufs + [dma((m,)) for m in (n, n, n, n, z, z, n, n, n, n)]
+
+
+def reduce_kernel(sizes, dims, top_ref, bot_ref, np_ref, g_ref, nu_ref, nd_ref, n6_ref, gs_ref, ssem, rsem, *rest):
+    place = Place(dims)
+    where, barrier, n = greet(place, sizes)
+    pl.semaphore_wait(barrier, n)
+    edges = send_edges(where, top_ref, bot_ref, np_ref, nu_ref, nd_ref, n6_ref, ssem, rsem)
+    sent = sum_devices(place, g_ref, gs_ref, *rest[:6], rest[6:])
     for c in edges:
         c.wait_recv()
-    for c in edges + first + second + third + fourth:
+    for c in edges + sent:
         c.wait_send()
 
 
@@ -422,7 +518,7 @@
     for tap in range(9):
         gm_ref[tap] = g_ref[G_MID + tap * WD : G_MID + (tap + 1) * WD].astype(F32)
         go_ref[tap] = g_ref[G_OUT + tap * CH : G_OUT + (tap + 1) * CH].astype(F32)
-        gi_ref[tap] = g_ref[G_IN + tap * CH : G_IN + (tap + 1) * CH].astype(F32).T
+        gi_ref[tap] = g_ref[G_IN + tap * CH : G_IN + (tap + 1) * CH].astype(F32)
 
 
 def sds(shape, dtype):
@@ -431,7 +527,7 @@
 
 def shards(sizes, fields, cotangent, kernel_in, kernel_mid, kernel_out, patch_anchors, blend_weights, tile_counts):
     nla, nlo = sizes
-    anch = patch_anchors[0, 0]
+    anch = patch_anchors.transpose(0, 1, 3, 2)[0, 0]
     dma = pltpu.SemaphoreType.DMA
     fc, edge, canv = pl.pallas_call(
         prep_kernel,
@@ -442,39 +538,32 @@
         scratch_shapes=[pltpu.VMEM((4, CH * TR, 128), F32)],
     )(anch, tile_counts, fields, cotangent, blend_weights)
 
-    up, dn, en, cn = pl.pallas_call(
+    up, dn, en, cn, win, wmid, wout, woutt, wmidt = pl.pallas_call(
         functools.partial(exchange_kernel, sizes),
         name="exchange",
         out_shape=(
             sds((MG, 2 * CH, TC), BF16), sds((MG, 2 * CH, TC), BF16),
             sds((6, 2 * CH, 128), BF16), sds((8, 2 * TR, EXT), BF16),
+            sds((2 * WD, 12 * CH), BF16), sds((2 * WD, 12 * WD), BF16), sds((6 * CH, 4 * WD), BF16),
+            sds((2 * WD, 12 * CH), BF16), sds((2 * WD, 12 * WD), BF16),
         ),
-        in_specs=vmem(3),
-        out_specs=vmem(4),
+        in_specs=vmem(6),
+        out_specs=vmem(9),
         scratch_shapes=[dma((16,)), dma((16,))],
         compiler_params=pltpu.CompilerParams(collective_id=0, has_side_effects=True),
-    )(fc, edge, canv)
-
-    def two_rows(w):
-        k = w.shape[1] // 3
-        return jnp.concatenate([jnp.pad(w, ((0, 0), (0, k))), jnp.pad(w, ((0, 0), (k, 0)))], axis=0)
-
-    win = two_rows(kernel_in.transpose(1, 0, 2).reshape(WD, 9 * CH))
-    wmid = two_rows(kernel_mid.transpose(1, 0, 2).reshape(WD, 9 * WD))
-    wout = two_rows(kernel_out.reshape(3, 3, CH, WD).transpose(1, 2, 0, 3).reshape(3 * CH, 3 * WD))
-    woutt = two_rows(kernel_out[::-1].transpose(2, 0, 1).reshape(WD, 9 * CH))
-    wmidt = two_rows(kernel_mid[::-1].transpose(2, 0, 1).reshape(WD, 9 * WD))
-
-    parts = -(-(G_END // 8) // nla)
-    pp = -(-parts // nlo)
-    grow = nla * parts * 8
+    )(fc, edge, canv, kernel_in.transpose(0, 2, 1), kernel_mid, kernel_out)
+
+    dims = (2, 4, 2, 8) if sizes == (16, 16) else (1, nla // 2, 1, nlo)
+    parts = dims[0] * dims[1] * dims[2]
+    rows = -(-G_END // (16 * parts)) * 8
+    grow = 2 * parts * rows
     vm = pltpu.VMEM
     num, top, bot, npk, grads, inv = pl.pallas_call(
         patch_kernel,
         name="patches",
         out_shape=(
             sds((TR, CH, TC), F32), sds((MG, CH, TC), BF16), sds((MG, CH, TC), BF16),
-            sds((CH, 128), BF16), sds((grow, WD), BF16), sds((TR, TC), F32),
+            sds((CH, 128), BF16), sds((grow, WD), F32), sds((TR, TC), F32),
         ),
         in_specs=smem(2) + vmem(12),
         out_specs=vmem(6),
@@ -487,34 +576,29 @@
     )(anch, tile_counts, fc, up, dn, en, canv, cn, blend_weights, win, wmid, wout, woutt, wmidt)
 
     nu, nd, n6, gs = pl.pallas_call(
-        functools.partial(reduce_kernel, sizes, parts),
+        functools.partial(reduce_kernel, sizes, dims),
         name="reduce",
         out_shape=(
             sds((MG, CH, TC), BF16), sds((MG, CH, TC), BF16), sds((6, CH, 128), BF16),
-            sds((nla, parts, 8, WD), BF16),
+            sds((2, parts, rows, WD), BF16),
         ),
         in_specs=vmem(4),
         out_specs=vmem(4),
-        scratch_shapes=[
-            vm((nla, parts, 8, WD), BF16), vm((nlo, pp, 8, WD), F32), vm((parts, 8, WD), F32),
-            vm((pp, 8, WD), BF16), vm((nlo * pp, 8, WD), BF16),
-            dma((8,)), dma((8,)), dma((nla,)), dma((nla,)), dma((nlo,)), dma((nlo,)),
-            dma((nlo,)), dma((nlo,)), dma((nla,)), dma((nla,)),
-        ],
+        scratch_shapes=[dma((8,)), dma((8,))] + sum_scratch(dims, rows),
         compiler_params=pltpu.CompilerParams(collective_id=1, has_side_effects=True),
-    )(top, bot, npk, grads.reshape(nla, parts, 8, WD))
+    )(top, bot, npk, grads.reshape(2, parts, rows, WD))
 
     blended, gi, gm, go = pl.pallas_call(
         finish_kernel,
         name="finish",
         out_shape=(
-            sds((CH * TR, TC), F32), sds((9, WD, CH), F32), sds((9, WD, WD), F32), sds((9, CH, WD), F32),
+            sds((CH * TR, TC), F32), sds((9, CH, WD), F32), sds((9, WD, WD), F32), sds((9, CH, WD), F32),
         ),
         in_specs=vmem(6),
         out_specs=vmem(4),
         scratch_shapes=[vm((2, CH * TR, 128), F32)],
     )(num, inv, nu, nd, n6, gs.reshape(grow, WD))
-    return blended.reshape(CH, TR, TC), gi, gm, go
+    return blended.reshape(CH, TR, TC), gi.transpose(0, 2, 1), gm, go
 
 
 def solution(mesh):

time: 86.3 us -> 71.8 us (0.83)
  local copies, waits for them, and re-layouts: 6.96 us -> 0 us
  Pallas kernels: 75 us -> 70.3 us
  other arithmetic: 2.85 us -> 0 us
    pallas_call x1, Pallas kernels: 31 us -> 25.5 us  [shards(): pl.pallas_call(functools.partial(reduce_kernel, sizes, dims), name='reduc...]
    concatenate x3 -> x0, other arithmetic: 2.85 us -> none  [two_rows(): jnp.concatenate([jnp.pad(w, ((0, 0), (0, k))), jnp.pad(w, ((0, 0), (k, 0)...]
    reshape x5 -> x0, local copies, waits for them, and re-layouts: 2.53 us -> none  [the longest x1 1 us: shards(): win = two_rows(kernel_in.transpose(1, 0, 2).reshape(WD, 9 * CH))]
    unnamed x5 -> x0, local copies, waits for them, and re-layouts: 2.17 us -> none
    squeeze x1 -> x0, local copies, waits for them, and re-layouts: 1.35 us -> none  [shards(): anch = patch_anchors[0, 0]]
    rev x2 -> x0, local copies, waits for them, and re-layouts: 0.91 us -> none  [the longest x1 0.89 us: shards(): woutt = two_rows(kernel_out[::-1].transpose(2, 0, 1).reshape(WD, 9 * CH))]
where the time goes in v3:
time: 71.8 us; the launch traced here: 71.6 us
  Pallas kernels  70.3 us (98%)
  between operations  1.29 us (2%)
    pallas_call x1, Pallas kernels, shards(): pl.pallas_call(functools.partial(reduce_kernel, sizes, dims), name='reduc...  25.5 us
    pallas_call x1, Pallas kernels, shards(): pl.pallas_call(patch_kernel, name='patches', out_shape=(sds((TR, CH, TC),...  22.1 us
    pallas_call x1, Pallas kernels, shards(): pl.pallas_call(functools.partial(exchange_kernel, sizes), name='exchange'...  18.5 us
    pallas_call x1, Pallas kernels, shards(): pl.pallas_call(finish_kernel, name='finish', out_shape=(sds((CH * TR, TC)...  2.37 us
    pallas_call x1, Pallas kernels, shards(): pl.pallas_call(prep_kernel, name='prepare', out_shape=(sds((TR, 2 * CH, T...  1.81 us

profile of v3, /device:TPU:1, one launch (start us, length us, event | category | flops | bytes accessed | tf_op | source)
XLA Modules:
  0.0 71.6 jit_solution(3073084331675628816)
XLA Ops:
  1.3 1.8 %prepare.1 = (bf16[8,64,256]{2,1,0:T(8,128)(2,1)}, bf16[64,128]{1,0:T(8,128)(2,1)}, bf16[16,384]{1,0:T(8,128)(2,1)}) custom-call(s32[2,4]{1,0:T(2,128)} %bitcast.11, s32[1,1]{1,0:T(1,128)S(6)} %copy.12.cnt, bf16[32,8,256]{2,1,0:T(8,128)(2,1)} %f_ref.1, bf16[32,8,256]{2,1,0:T(8,128)(2,1)} %c_ref.1, s32[4,8,256]{2,1,0:T(8,128)} %w_ref.3), custom_call_target="tpu_custom_call" | custom-call | tf_op jit(solution)/shard_map/prepare/pallas_call | solution.py:532
  3.1 18.5 %exchange.1 = (bf16[4,64,256]{2,1,0:T(8,128)(2,1)}, bf16[4,64,256]{2,1,0:T(8,128)(2,1)}, bf16[6,64,128]{2,1,0:T(8,128)(2,1)}, bf16[8,16,384]{2,1,0:T(8,128)(2,1)...) custom-call(bf16[8,64,256]{2,1,0:T(8,128)(2,1)} %get-tuple-element.3, ...), custom_call_target="tpu_custom_call" | custom-call | tf_op jit(solution)/shard_map/exchange/pallas_call | solution.py:541
  21.5 22.1 %patches.1 = (f32[8,32,256]{2,1,0:T(8,128)}, bf16[4,32,256]{2,1,0:T(8,128)(2,1)}, bf16[4,32,256]{2,1,0:T(8,128)(2,1)}, bf16[32,128]{1,0:T(8,128)(2,1)}, f32[1792,128]{1,0:T(8,128)}, /*index=5*/f32[8,256]{1,0:T(8,128)}) custom-call(s32[2,4]{1,0:T(2,128)} %bitcast.12, s32[1,1]{1,0:T(1,128)S(6)} %copy.12.cnt, bf16[8,64,256]{2,1,0:T(8,128)(2,1)} %get-tuple-element.30.fc_ref, ...), custom_call_target="tpu_custom_call" | custom-call | tf_op jit(solution)/shard_map/patches/pallas_call | solution.py:561
  43.7 25.5 %reduce.1 = (bf16[4,32,256]{2,1,0:T(8,128)(2,1)}, bf16[4,32,256]{2,1,0:T(8,128)(2,1)}, bf16[6,32,128]{2,1,0:T(8,128)(2,1)}, bf16[2,16,56,128]{3,2,1,0:T(8,128)(2,1)}) custom-call(bf16[4,32,256]{2,1,0:T(8,128)(2,1)} %get-tuple-element.44.top_ref, bf16[4,32,256]{2,1,0:T(8,128)(2,1)} %get-tuple-element.45.bot_ref, bf16[32,128]{1,0:T(8,128)(2,1)} %get-tuple-element.46.np_ref, ...), custom_call_target="tpu_custom_call" | custom-call | tf_op jit(solution)/shard_map/reduce/pallas_call | solution.py:578
  69.2 2.4 %finish.1 = (f32[256,256]{1,0:T(8,128)}, f32[9,32,128]{2,1,0:T(8,128)}, f32[9,128,128]{2,1,0:T(8,128)}, f32[9,32,128]{2,1,0:T(8,128)}) custom-call(f32[8,32,256]{2,1,0:T(8,128)} %get-tuple-element.42.num_ref, f32[8,256]{1,0:T(8,128)} %get-tuple-element.43.inv_ref, bf16[4,32,256]{2,1,0:T(8,128)(2,1)} %get-tuple-element.48.nu_ref, ...), custom_call_target="tpu_custom_call" | custom-call | tf_op jit(solution)/shard_map/finish/pallas_call | solution.py:591

commit v4 on v3

--- a/solution.py
+++ b/solution.py
@@ -39,7 +39,7 @@
     return lax.broadcasted_iota(jnp.int32, shape, len(shape) - 1)
 
 
-def prep_kernel(anch, cnt, f_ref, c_ref, w_ref, fc_ref, e_ref, cv_ref, scr):
+def prepare(anch, cnt, f_ref, c_ref, w_ref, fc_ref, e_ref, cv_ref, scr):
     for half in range(2):
         at = slice(half * 128, half * 128 + 128)
         scr[half] = f_ref[:, :, at].astype(F32).reshape(CH * TR, 128)
@@ -83,14 +83,9 @@
         one, two = two_rows(jnp.concatenate(taps, axis=0))
         dst[0:WD] = one.T
         dst[WD : 2 * WD] = two.T
-    zero = jnp.zeros((WD, 3 * WD), BF16)
-    for dst in (wmid_ref, wmidt_ref):
-        dst[0:WD, 9 * WD :] = zero
-        dst[WD : 2 * WD, : 3 * WD] = zero
     for t in range(9):
-        for dst, w in ((wmid_ref, km_ref[t]), (wmidt_ref, km_ref[8 - t].T)):
-            dst[0:WD, t * WD : (t + 1) * WD] = w
-            dst[WD : 2 * WD, (t + 3) * WD : (t + 4) * WD] = w
+        wmid_ref[:, t * WD : (t + 1) * WD] = km_ref[t]
+        wmidt_ref[:, t * WD : (t + 1) * WD] = km_ref[8 - t].T
     zero = jnp.zeros((CH, WD), BF16)
     for ro in range(2):
         for dx in range(3):
@@ -101,8 +96,8 @@
 
 
 def exchange_kernel(
-    sizes, fc_ref, e_ref, cv_ref, ki_ref, km_ref, ko_ref, up_ref, dn_ref, en_ref, cn_ref,
-    win_ref, wmid_ref, wout_ref, woutt_ref, wmidt_ref, ssem, rsem,
+    sizes, anch, cnt, f_ref, c_ref, w_ref, ki_ref, km_ref, ko_ref, fc_ref, cv_ref, up_ref, dn_ref, en_ref, cn_ref,
+    win_ref, wmid_ref, wout_ref, woutt_ref, wmidt_ref, e_ref, scr, ssem, rsem,
 ):
     la, lo = lax.axis_index("lat"), lax.axis_index("lon")
     nla, nlo = sizes
@@ -110,6 +105,7 @@
     barrier = pltpu.get_barrier_semaphore()
     for dev in where:
         pl.semaphore_signal(barrier, inc=1, device_id=dev, device_id_type=MESH)
+    prepare(anch, cnt, f_ref, c_ref, w_ref, fc_ref, e_ref, cv_ref, scr)
     pl.semaphore_wait(barrier, len(NB))
     copies = []
 
@@ -151,8 +147,18 @@
     buf[2 * ch : 3 * ch, at] = shift_cols(x, 1)
 
 
+def put_two(buf, r, x, ch):
+    at = slice((r + 1) * TC, (r + 2) * TC)
+    buf[0:ch, at] = shift_cols(x, -1)
+    buf[ch : 2 * ch, at] = x
+
+
 def four_rows(buf, i, rows=slice(None)):
     return jnp.concatenate([buf[rows, (2 * i + j) * TC : (2 * i + j + 1) * TC] for j in range(4)], axis=0)
+
+
+def three_rows(buf, r):
+    return jnp.concatenate([buf[:, (r + j) * TC : (r + j + 1) * TC] for j in range(3)], axis=0)
 
 
 def dot(a, b):
@@ -257,19 +263,18 @@
                 sl1[:, at(r)] = s + h * (1.0 - s)
 
         def second(i):
-            zz = dot(wmid_ref[...], four_rows(h1b, i))
             gg = dot(woutt_ref[...], four_rows(dpb, i))
             for r in rows(i):
-                z, g = half(zz, r), half(gg, r)
+                z, g = dot(wmid_ref[...], three_rows(h1b, r)), half(gg, r)
                 t = jnp.tanh(0.5 * z)
                 s = 0.5 + 0.5 * t
                 h = z * s
-                h2b[:, at(r + 1)] = (h1b[WD : 2 * WD, at(r + 1)].astype(F32) + h).astype(BF16)
+                put_two(h2b, r, (h1b[WD : 2 * WD, at(r + 1)].astype(F32) + h).astype(BF16), WD)
                 dh2[:, at(r)] = g
                 put_shifted(dzb, r, (g * (s + h * (1.0 - s))).astype(BF16), WD)
 
         def blend(i):
-            oo = dot(wout_ref[...], four_rows(h2b, i))
+            oo = dot(wout_ref[...], four_rows(h2b, i, slice(WD, 2 * WD)))
             for r in rows(i):
                 v = half(oo, r)
                 o = shift_cols(v[0:CH], -1) + v[CH : 2 * CH] + shift_cols(v[2 * CH :], 1)
@@ -278,10 +283,9 @@
                 canvas[a + r] += pltpu.roll(o, place, 1)
 
         def third(i):
-            zz = dot(wmidt_ref[...], four_rows(dzb, i))
             for r in rows(i):
-                g = dh2[:, at(r)] + half(zz, r)
-                dz1[:, at(r)] = (g * sl1[:, at(r)]).astype(BF16)
+                g = dh2[:, at(r)] + dot(wmidt_ref[...], three_rows(dzb, r))
+                put_two(dz1, r, (g * sl1[:, at(r)]).astype(BF16), WD)
 
         window(0)
         window(1)
@@ -304,13 +308,19 @@
         third(3)
         blend(3)
 
-        hh = h2b[:, TC : TC + CELLS]
-        d1 = dz1[...]
-        d2 = dzb[0 : 2 * WD, TC : TC + CELLS]
-        for dy in range(3):
-            gmid[dy] += dot_t(d2, h1b[0 : 2 * WD, dy * TC : dy * TC + CELLS])
-            gout[dy] += dot_t(dpb[:, (2 - dy) * TC : (2 - dy) * TC + CELLS], hh)
-            gin[dy] += dot_t(xpb[:, dy * TC : dy * TC + CELLS], d1)
+        def slab(buf, n, row):
+            return buf[0:n, row * TC : row * TC + CELLS]
+
+        gmid[...] += dot_t(
+            dzb[WD : 2 * WD, TC : TC + CELLS],
+            jnp.concatenate([slab(h1b, 3 * WD, dy) for dy in range(3)], axis=0),
+        )
+        gout[...] += dot_t(
+            jnp.concatenate([slab(dpb, 2 * CH, 2 - dy) for dy in range(3)], axis=0), slab(h2b, 2 * WD, 1)
+        )
+        gin[...] += dot_t(
+            jnp.concatenate([slab(xpb, 2 * CH, dy) for dy in range(3)], axis=0), slab(dz1, 2 * WD, 1)
+        )
         return carry
 
     lax.fori_loop(0, cnt[0, 0], one_patch, 0)
@@ -332,13 +342,13 @@
     np_ref[...] = pk.astype(BF16)
     for tap in range(9):
         dy, dx = divmod(tap, 3)
+        g_ref[G_MID + tap * WD : G_MID + (tap + 1) * WD] = gmid[:, tap * WD : (tap + 1) * WD]
         ro, co = ((1, 0), (1, 1), (0, 1))[dx]
-        g_ref[G_MID + tap * WD : G_MID + (tap + 1) * WD] = gmid[
-            dy, ro * WD : (ro + 1) * WD, co * WD : (co + 1) * WD
-        ]
-        s = 2 - dx
-        g_ref[G_OUT + tap * CH : G_OUT + (tap + 1) * CH] = gout[dy, s * CH : (s + 1) * CH]
-        g_ref[G_IN + tap * CH : G_IN + (tap + 1) * CH] = gin[dy, dx * CH : (dx + 1) * CH]
+        at = (2 * dy + ro) * CH
+        g_ref[G_OUT + tap * CH : G_OUT + (tap + 1) * CH] = gout[at : at + CH, co * WD : (co + 1) * WD]
+        ro, co = ((0, 1), (1, 1), (1, 0))[dx]
+        at = (2 * dy + ro) * CH
+        g_ref[G_IN + tap * CH : G_IN + (tap + 1) * CH] = gin[at : at + CH, co * WD : (co + 1) * WD]
     if g_ref.shape[0] > G_END:
         g_ref[G_END:] = jnp.zeros((g_ref.shape[0] - G_END, WD), F32)
 
@@ -529,29 +539,23 @@
     nla, nlo = sizes
     anch = patch_anchors.transpose(0, 1, 3, 2)[0, 0]
     dma = pltpu.SemaphoreType.DMA
-    fc, edge, canv = pl.pallas_call(
-        prep_kernel,
-        name="prepare",
-        out_shape=(sds((TR, 2 * CH, TC), BF16), sds((2 * CH, 128), BF16), sds((2 * TR, EXT), BF16)),
-        in_specs=smem(2) + vmem(3),
-        out_specs=vmem(3),
-        scratch_shapes=[pltpu.VMEM((4, CH * TR, 128), F32)],
-    )(anch, tile_counts, fields, cotangent, blend_weights)
-
-    up, dn, en, cn, win, wmid, wout, woutt, wmidt = pl.pallas_call(
+    fc, canv, up, dn, en, cn, win, wmid, wout, woutt, wmidt = pl.pallas_call(
         functools.partial(exchange_kernel, sizes),
         name="exchange",
         out_shape=(
+            sds((TR, 2 * CH, TC), BF16), sds((2 * TR, EXT), BF16),
             sds((MG, 2 * CH, TC), BF16), sds((MG, 2 * CH, TC), BF16),
             sds((6, 2 * CH, 128), BF16), sds((8, 2 * TR, EXT), BF16),
-            sds((2 * WD, 12 * CH), BF16), sds((2 * WD, 12 * WD), BF16), sds((6 * CH, 4 * WD), BF16),
-            sds((2 * WD, 12 * CH), BF16), sds((2 * WD, 12 * WD), BF16),
+            sds((2 * WD, 12 * CH), BF16), sds((WD, 9 * WD), BF16), sds((6 * CH, 4 * WD), BF16),
+            sds((2 * WD, 12 * CH), BF16), sds((WD, 9 * WD), BF16),
         ),
-        in_specs=vmem(6),
-        out_specs=vmem(9),
-        scratch_shapes=[dma((16,)), dma((16,))],
+        in_specs=smem(2) + vmem(6),
+        out_specs=vmem(11),
+        scratch_shapes=[
+            pltpu.VMEM((2 * CH, 128), BF16), pltpu.VMEM((4, CH * TR, 128), F32), dma((16,)), dma((16,)),
+        ],
         compiler_params=pltpu.CompilerParams(collective_id=0, has_side_effects=True),
-    )(fc, edge, canv, kernel_in.transpose(0, 2, 1), kernel_mid, kernel_out)
+    )(anch, tile_counts, fields, cotangent, blend_weights, kernel_in.transpose(0, 2, 1), kernel_mid, kernel_out)
 
     dims = (2, 4, 2, 8) if sizes == (16, 16) else (1, nla // 2, 1, nlo)
     parts = dims[0] * dims[1] * dims[2]
@@ -570,8 +574,8 @@
         scratch_shapes=[
             vm((2 * TR, 2 * CH, EXT), BF16), vm((2 * TR, EXT), F32),
             vm((3 * CH, PAD), BF16), vm((3 * CH, PAD), BF16), vm((3 * WD, PAD), BF16), vm((3 * WD, PAD), BF16),
-            vm((WD, PAD), BF16), vm((WD, CELLS), F32), vm((WD, CELLS), F32), vm((WD, CELLS), BF16),
-            vm((2 * TR, CH, EXT), F32), vm((3, 2 * WD, 2 * WD), F32), vm((3, 3 * CH, WD), F32), vm((3, 3 * CH, WD), F32),
+            vm((2 * WD, PAD), BF16), vm((WD, CELLS), F32), vm((WD, CELLS), F32), vm((2 * WD, PAD), BF16),
+            vm((2 * TR, CH, EXT), F32), vm((WD, 9 * WD), F32), vm((6 * CH, 2 * WD), F32), vm((6 * CH, 2 * WD), F32),
         ],
     )(anch, tile_counts, fc, up, dn, en, canv, cn, blend_weights, win, wmid, wout, woutt, wmidt)
 

time: 71.8 us -> 69.8 us (0.972)
  Pallas kernels: 70.3 us -> 68.3 us
    pallas_call x1 -> x0, Pallas kernels: 1.81 us -> none  [shards(): pl.pallas_call(prep_kernel, name='prepare', out_shape=(sds((TR, 2 * CH, T...]
where the time goes in v4:
time: 69.8 us; the launch traced here: 69.6 us
  Pallas kernels  68.3 us (98%)
  between operations  1.3 us (2%)
    pallas_call x1, Pallas kernels, shards(): pl.pallas_call(functools.partial(reduce_kernel, sizes, dims), name='reduc...  25.5 us
    pallas_call x1, Pallas kernels, shards(): pl.pallas_call(patch_kernel, name='patches', out_shape=(sds((TR, CH, TC),...  21.9 us
    pallas_call x1, Pallas kernels, shards(): pl.pallas_call(functools.partial(exchange_kernel, sizes), name='exchange'...  18.5 us
    pallas_call x1, Pallas kernels, shards(): pl.pallas_call(finish_kernel, name='finish', out_shape=(sds((CH * TR, TC)...  2.37 us

profile of v4, /device:TPU:1, one launch (start us, length us, event | category | flops | bytes accessed | tf_op | source)
XLA Modules:
  0.0 69.6 jit_solution(14307142363069228678)
XLA Ops:
  1.3 18.5 %exchange.1 = (bf16[8,64,256]{2,1,0:T(8,128)(2,1)}, bf16[16,384]{1,0:T(8,128)(2,1)}, bf16[4,64,256]{2,1,0:T(8,128)(2,1)}, bf16[4,64,256]{2,1,0:T(8,128)(2,1)}, b...) custom-call(s32[2,4]{1,0:T(2,128)} %bitcast.11, ...), custom_call_target="tpu_custom_call" | custom-call | tf_op jit(solution)/shard_map/exchange/pallas_call | solution.py:542
  19.8 21.9 %patches.1 = (f32[8,32,256]{2,1,0:T(8,128)}, bf16[4,32,256]{2,1,0:T(8,128)(2,1)}, bf16[4,32,256]{2,1,0:T(8,128)(2,1)}, bf16[32,128]{1,0:T(8,128)(2,1)}, f32[1792,128]{1,0:T(8,128)}, /*index=5*/f32[8,256]{1,0:T(8,128)}) custom-call(s32[2,4]{1,0:T(2,128)} %bitcast.12, s32[1,1]{1,0:T(1,128)S(6)} %copy.12.cnt, bf16[8,64,256]{2,1,0:T(8,128)(2,1)} %get-tuple-element.29.fc_ref, ...), custom_call_target="tpu_custom_call" | custom-call | tf_op jit(solution)/shard_map/patches/pallas_call | solution.py:565
  41.7 25.5 %reduce.1 = (bf16[4,32,256]{2,1,0:T(8,128)(2,1)}, bf16[4,32,256]{2,1,0:T(8,128)(2,1)}, bf16[6,32,128]{2,1,0:T(8,128)(2,1)}, bf16[2,16,56,128]{3,2,1,0:T(8,128)(2,1)}) custom-call(bf16[4,32,256]{2,1,0:T(8,128)(2,1)} %get-tuple-element.42.top_ref, bf16[4,32,256]{2,1,0:T(8,128)(2,1)} %get-tuple-element.43.bot_ref, bf16[32,128]{1,0:T(8,128)(2,1)} %get-tuple-element.44.np_ref, ...), custom_call_target="tpu_custom_call" | custom-call | tf_op jit(solution)/shard_map/reduce/pallas_call | solution.py:582
  67.2 2.4 %finish.1 = (f32[256,256]{1,0:T(8,128)}, f32[9,32,128]{2,1,0:T(8,128)}, f32[9,128,128]{2,1,0:T(8,128)}, f32[9,32,128]{2,1,0:T(8,128)}) custom-call(f32[8,32,256]{2,1,0:T(8,128)} %get-tuple-element.40.num_ref, f32[8,256]{1,0:T(8,128)} %get-tuple-element.41.inv_ref, bf16[4,32,256]{2,1,0:T(8,128)(2,1)} %get-tuple-element.46.nu_ref, ...), custom_call_target="tpu_custom_call" | custom-call | tf_op jit(solution)/shard_map/finish/pallas_call | solution.py:595
